TPU v7x, 32 devices: a whole 2x2x4 slice. The times are simulated.
32 devices in a mesh: member: 2 (over x), wide: 16 (over z, y, core).
Axes of the slice: x: 2, y: 2, z: 4, core: 2. Of those that a mesh axis runs over, the one named last changes fastest.
Arguments:
- stream_now: float32 [4, 256, 4096], P('member', 'wide'), parts along dimension 0, may hold values from -6 to 6
- vorticity: float32 [4, 256, 4096], P('member', 'wide'), parts along dimension 0, may hold values from -0.62 to 0.62
Outputs:
- vorticity_next: float32 [4, 256, 4096], P('member', 'wide'), parts along dimension 0
- stream_next: float32 [4, 256, 4096], P('member', 'wide'), parts along dimension 0
There are 2 independent parts, one for each index of `member`. A program takes and returns all parts, laid end to end along the dimension named above; each array names one. Nothing has to cross between parts.
All inputs are finite; a program needn't handle non-finite values.
Results may differ from a plain program's by a relative error of at most 0.00002.
Values sent between devices are 32-bit elements; how exact they have to be, the bound alone decides.
No kernel may reach another device: no remote copies, remote signals or barrier semaphores. Data moves between devices by JAX's collectives and lax.ppermute only.
A program may use at most 128 MiB of HBM per device.

v0:
```python
import functools

import jax
import jax.numpy as jnp
from jax import lax
from jax.experimental import pallas as pl
from jax.experimental.pallas import tpu as pltpu
from jax.sharding import PartitionSpec as P


LANES = 128
SUBS = 8
HALO = 3
MID_HALO = 6
TWO_HALO = 4
RELAX = 0.8
COUPLING = (0.02, 0.04)
TIME_STEP = 0.5
BETA = 0.05
DRAG = (0.0, 0.02)
COARSE_SWEEPS = 8


class Level:
    def __init__(self, level, tiles, stride):
        h2 = (2.0**level) ** 2
        self.tiles, self.stride = tiles, stride
        diag = [4.0 / h2 + f for f in COUPLING]
        self.keep = 1.0 - RELAX
        self.near = [RELAX / (d * h2) for d in diag]
        self.other = [RELAX * f / d for f, d in zip(COUPLING, diag)]
        self.src = [RELAX / d for d in diag]
        self.diag = diag
        self.inv_h2 = 1.0 / h2
        self.size = tiles * SUBS


def lane_index():
    return lax.broadcasted_iota(jnp.int32, (SUBS, LANES), 1)


def at(level, row, tile=0):
    base = row * level.size
    if not isinstance(row, int):
        base = pl.multiple_of(base, SUBS)
    return pl.ds(base + tile * SUBS, SUBS)


def load(ref, level, layer, row):
    return [ref[layer, at(level, row, t), :] for t in range(level.tiles)]


def store(ref, level, layer, row, values):
    for t in range(level.tiles):
        ref[layer, at(level, row, t), :] = values[t]


def east(values, stride=1):
    rolled = [pltpu.roll(v, LANES - stride, 1) for v in values]
    after = rolled[1:] + [pltpu.roll(rolled[0], SUBS - 1, 0)]
    edge = lane_index() >= LANES - stride
    return [jnp.where(edge, a, r) for a, r in zip(after, rolled)]


def west(values, stride=1):
    rolled = [pltpu.roll(v, stride, 1) for v in values]
    before = [pltpu.roll(rolled[-1], 1, 0)] + rolled[:-1]
    edge = lane_index() < stride
    return [jnp.where(edge, b, r) for b, r in zip(before, rolled)]


def transpose_tiles(tiles):
    sub = lax.broadcasted_iota(jnp.int32, (SUBS, LANES), 0)
    for k in (1, 2, 4):
        keep = (sub & k) == 0
        out = list(tiles)
        for i in range(SUBS):
            if not i & k:
                a, b = tiles[i], tiles[i + k]
                out[i] = jnp.where(keep, a, pltpu.roll(b, k, 0))
                out[i + k] = jnp.where(keep, pltpu.roll(a, SUBS - k, 0), b)
        tiles = out
    return tiles


def column_of(level, t, s):
    first = (s * level.tiles + t) * LANES
    return slice(first, first + LANES)


def to_native(level, dst, dst_row, src, layer, src_row, sign=1):
    for t in range(level.tiles):
        tiles = [src[layer, at(level, src_row + r, t), :] for r in range(SUBS)]
        for s, tile in enumerate(transpose_tiles(tiles)):
            dst[layer, dst_row : dst_row + SUBS, column_of(level, t, s)] = (
                tile if sign > 0 else -tile
            )


def row_blocks(low, high, block, body):
    count = high - low if isinstance(low, int) else high
    whole = count // block
    if whole > 1:
        lax.fori_loop(0, whole, lambda i, c: (body(low + i * block, block), c)[1], 0)
    elif whole == 1:
        body(low, block)
    if count % block:
        body(low + whole * block, count % block)


def star(rows, k, layer, level):
    centre = rows[k][layer]
    e, w = east(centre, level.stride), west(centre, level.stride)
    return [
        (n + s) + (a + b)
        for n, s, a, b in zip(rows[k + 1][layer], rows[k - 1][layer], e, w)
    ]


def load_rows(ref, level, first, count, margin=1):
    return {
        k: [load(ref, level, layer, first + k) for layer in range(2)]
        for k in range(-margin, count + margin)
    }


def sweep_rows(level, rows, source, count):
    out = {}
    for k in range(count):
        out[k] = []
        for layer in range(2):
            near = star(rows, k, layer, level)
            out[k].append(
                [
                    (level.keep * c + level.near[layer] * n)
                    + (level.other[layer] * o + level.src[layer] * b)
                    for c, n, o, b in zip(
                        rows[k][layer], near, rows[k][1 - layer], source[k][layer]
                    )
                ]
            )
    return out


def residual_rows(level, rows, source, count):
    out = {}
    for k in range(count):
        out[k] = []
        for layer in range(2):
            near = star(rows, k, layer, level)
            out[k].append(
                [
                    (b - level.diag[layer] * c)
                    + (level.inv_h2 * n + COUPLING[layer] * o)
                    for c, n, o, b in zip(
                        rows[k][layer], near, rows[k][1 - layer], source[k][layer]
                    )
                ]
            )
    return out


def store_rows(ref, level, first, rows, count):
    for k in range(count):
        for layer in range(2):
            store(ref, level, layer, first + k, rows[k][layer])


def sweep(level, dst, dst_at, src, src_at, b, b_at, low, high, block):
    def body(first, count):
        rows = load_rows(src, level, first + src_at, count)
        source = load_rows(b, level, first + b_at, count, 0)
        store_rows(dst, level, first + dst_at, sweep_rows(level, rows, source, count), count)

    row_blocks(low, high, block, body)


def start(level, dst, dst_at, b, b_at, low, high, block):
    def body(first, count):
        source = load_rows(b, level, first + b_at, count, 0)
        out = {
            k: [[level.src[l] * x for x in source[k][l]] for l in range(2)]
            for k in range(count)
        }
        store_rows(dst, level, first + dst_at, out, count)

    row_blocks(low, high, block, body)


def pack_columns(values):
    lane = lane_index()
    pick = (2 * lane) % LANES
    sums = [v + pltpu.roll(v, LANES - 1, 1) for v in values]
    picked = [jnp.take_along_axis(s, pick, axis=1) for s in sums]
    return [
        jnp.where(lane < LANES // 2, picked[2 * t], picked[2 * t + 1])
        for t in range(len(values) // 2)
    ]


def spread_columns(values):
    lane = lane_index()
    out = []
    for v in values:
        out.append(jnp.take_along_axis(v, lane // 2, axis=1))
        out.append(jnp.take_along_axis(v, LANES // 2 + lane // 2, axis=1))
    return out


def merge_columns(values, stride):
    even = (lane_index() // stride) % 2 == 0
    return [
        v + jnp.where(even, pltpu.roll(v, LANES - stride, 1), pltpu.roll(v, stride, 1))
        for v in values
    ]


def restrict(fine, dst, dst_at, coarse, src, src_at, b, b_at, low, high, block):
    def body(first, count):
        rows = load_rows(src, fine, 2 * first + src_at, 2 * count)
        source = load_rows(b, fine, 2 * first + b_at, 2 * count, 0)
        res = residual_rows(fine, rows, source, 2 * count)
        out = {}
        for k in range(count):
            out[k] = []
            for layer in range(2):
                pair = [x + y for x, y in zip(res[2 * k][layer], res[2 * k + 1][layer])]
                if coarse.tiles < fine.tiles:
                    pair = pack_columns(pair)
                else:
                    pair = merge_columns(pair, fine.stride)
                out[k].append([0.25 * x for x in pair])
        store_rows(dst, coarse, first + dst_at, out, count)

    row_blocks(low, high, block, body)


def correct(fine, coarse, dst, dst_at, src, src_at, add, add_at, low, high, block):
    def body(first, count):
        coarse_rows = load_rows(add, coarse, first + add_at, count, 0)
        fine_rows = load_rows(src, fine, 2 * first + src_at, 2 * count, 0)
        out = {}
        for k in range(count):
            spread = [
                spread_columns(v) if coarse.tiles < fine.tiles else v for v in coarse_rows[k]
            ]
            for half in range(2):
                out[2 * k + half] = [
                    [x + y for x, y in zip(fine_rows[2 * k + half][l], spread[l])]
                    for l in range(2)
                ]
        store_rows(dst, fine, 2 * first + dst_at, out, 2 * count)

    row_blocks(low, high, block, body)


def clear(ref, level, low, high):
    ref[:, low * level.size : high * level.size, :] = jnp.zeros(
        (ref.shape[0], (high - low) * level.size, LANES), jnp.float32
    )


def place():
    me, count = lax.axis_index("wide"), lax.axis_size("wide")
    return me, lax.rem(me, 2), me == 0, me == count - 1


def pack_kernel(level, rows, p_ref, q_ref, ext_ref, near_ref, far_ref, native, sems):
    copies = []
    for field, ref in enumerate((p_ref, q_ref)):
        for layer in range(2):
            which = 2 * field + layer
            copies.append(
                pltpu.make_async_copy(ref.at[layer], native.at[which], sems.at[which])
            )
            copies[-1].start()
    for which in range(4):
        copies[which].wait()
        for group in range(rows // SUBS):
            for t in range(level.tiles):
                tiles = [
                    native[which, group * SUBS : (group + 1) * SUBS, column_of(level, t, s)]
                    for s in range(SUBS)
                ]
                for r, tile in enumerate(transpose_tiles(tiles)):
                    ext_ref[which, at(level, HALO + group * SUBS + r, t), :] = tile
    send_edges(level, HALO, HALO, rows, ext_ref, near_ref, far_ref)


def send_edges(level, width, src_at, rows, src, near_ref, far_ref):
    _, odd, _, _ = place()
    size = width * level.size
    last = (src_at + rows - width) * level.size
    top = src_at * level.size
    near = pl.multiple_of(jnp.where(odd == 1, top, last), SUBS)
    far = pl.multiple_of(jnp.where(odd == 1, last, top), SUBS)
    near_ref[:, 0:size, :] = src[:, pl.ds(near, size), :]
    far_ref[:, 0:size, :] = src[:, pl.ds(far, size), :]


def receive_edges(level, width, dst_at, rows, dst, near_ref, far_ref):
    _, odd, first, last = place()
    size = width * level.size
    low = (dst_at + rows) * level.size
    top = (dst_at - width) * level.size
    near = pl.multiple_of(jnp.where(odd == 1, top, low), SUBS)
    far = pl.multiple_of(jnp.where(odd == 1, low, top), SUBS)
    dst[:, pl.ds(near, size), :] = near_ref[:, 0:size, :]
    outside = jnp.logical_or(first, last)
    dst[:, pl.ds(far, size), :] = jnp.where(outside, 0.0, far_ref[:, 0:size, :])


def shift_rows(level, ext, e_ref, w_ref, low, high, block):
    def body(first, count):
        for k in range(count):
            for f in range(4):
                v = load(ext, level, f, first + k)
                store(e_ref, level, f, first + k, east(v))
                store(w_ref, level, f, first + k, west(v))

    row_blocks(low, high, block, body)


def advance_rows(level, b_ref, ext, e_ref, w_ref, low, high, block):
    def body(first, count):
        for layer in range(2):
            for t in range(level.tiles):
                def grab(ref, field):
                    return {
                        k: ref[2 * field + layer, at(level, first + k, t), :]
                        for k in range(-1, count + 1)
                    }

                p, pe, pw = grab(ext, 0), grab(e_ref, 0), grab(w_ref, 0)
                q, qe, qw = grab(ext, 1), grab(e_ref, 1), grab(w_ref, 1)
                zonal = {k: pe[k] - pw[k] for k in p}
                for k in range(count):
                    n, s = k + 1, k - 1
                    v0, ve, vw = p[n] - p[s], pe[n] - pe[s], pw[n] - pw[s]
                    jac = q[n] * (zonal[k] + zonal[n]) - q[s] * (zonal[k] + zonal[s])
                    jac = jac - qe[k] * (v0 + ve) + qw[k] * (v0 + vw)
                    jac = jac + qe[n] * (pe[k] - p[n]) - qe[s] * (pe[k] - p[s])
                    jac = jac - qw[n] * (pw[k] - p[n]) + qw[s] * (pw[k] - p[s])
                    step = (TIME_STEP / 12.0) * jac + (0.5 * TIME_STEP * BETA) * zonal[k]
                    if layer == 1:
                        lap = (p[n] + p[s]) + (pe[k] + pw[k]) - 4.0 * p[k]
                        step = step + (TIME_STEP * DRAG[1]) * lap
                    b_ref[layer, at(level, first + k, t), :] = step - q[k]

    row_blocks(low, high, block, body)


def inner_kernel(level, coarse, rows, ext, e_ref, w_ref, b_ref, v_one, v_two, bc_ref):
    low, high = HALO, HALO + rows
    shift_rows(level, ext, e_ref, w_ref, low, high, 4)
    advance_rows(level, b_ref, ext, e_ref, w_ref, low + 1, high - 1, 2)
    sweep(level, v_one, 0, ext, 0, b_ref, 0, low + 2, high - 2, 4)
    sweep(level, v_two, 0, v_one, 0, b_ref, 0, low + 3, high - 3, 4)
    restrict(level, bc_ref, 0, coarse, v_two, HALO, b_ref, HALO, 2, rows // 2 - 2, 2)


def outer_kernel(level, coarse, rows, *refs):
    near_ref, far_ref = refs[7:9]
    ext, e_ref, w_ref, b_ref, v_one, v_two, bc_ref, bc_near_ref, bc_far_ref = refs[9:]
    _, _, is_first, is_last = place()
    low, high = HALO, HALO + rows
    total = rows + 2 * HALO
    receive_edges(level, HALO, HALO, rows, ext, near_ref, far_ref)
    shift_rows(level, ext, e_ref, w_ref, 0, low, 3)
    shift_rows(level, ext, e_ref, w_ref, high, total, 3)
    advance_rows(level, b_ref, ext, e_ref, w_ref, 1, low + 1, 3)
    advance_rows(level, b_ref, ext, e_ref, w_ref, high - 1, total - 1, 3)
    sweep(level, v_one, 0, ext, 0, b_ref, 0, 1, low + 2, 4)
    sweep(level, v_one, 0, ext, 0, b_ref, 0, high - 2, total - 1, 4)

    def trim(ref):
        @pl.when(is_first)
        def _():
            clear(ref, level, 0, HALO)

        @pl.when(is_last)
        def _():
            clear(ref, level, high, total)

    trim(v_one)
    sweep(level, v_two, 0, v_one, 0, b_ref, 0, 2, low + 3, 4)
    sweep(level, v_two, 0, v_one, 0, b_ref, 0, high - 3, total - 2, 4)
    trim(v_two)
    half = rows // 2
    restrict(level, bc_ref, 0, coarse, v_two, HALO, b_ref, HALO, 0, 2, 2)
    restrict(level, bc_ref, 0, coarse, v_two, HALO, b_ref, HALO, half - 2, half, 2)
    send_edges(coarse, MID_HALO, 0, half, bc_ref, bc_near_ref, bc_far_ref)


def emit_kernel(level, rows, b_ref, next_ref, native, sems):
    copies = []
    for layer in range(2):
        for group in range(rows // SUBS):
            rows_of = pl.ds(group * SUBS, SUBS)
            to_native(level, native, group * SUBS, b_ref, layer, HALO + group * SUBS, -1)
            copies.append(
                pltpu.make_async_copy(
                    native.at[layer, rows_of], next_ref.at[layer, rows_of],
                    sems.at[layer, group],
                )
            )
            copies[-1].start()
    for copy in copies:
        copy.wait()


def middle_kernel(
    fine, level, two, three, rows, b_own, near_ref, far_ref, v0_ref,
    b_ref, v_ref, b2_ref, v2_ref, out_ref, two_near_ref, two_far_ref,
    v_one, w_two, b3,
):
    _, odd, is_first, is_last = place()
    total = rows + 2 * MID_HALO
    own = rows // 2
    edge = MID_HALO * level.size
    b_ref[:, edge : edge + rows * level.size, :] = b_own[...]
    receive_edges(level, MID_HALO, MID_HALO, rows, b_ref, near_ref, far_ref)
    start(level, v_one, 0, b_ref, 0, 0, total, 4)

    def trim(ref, of, halo, n):
        @pl.when(is_first)
        def _():
            clear(ref, of, 0, halo)

        @pl.when(is_last)
        def _():
            clear(ref, of, halo + n, 2 * halo + n)

    trim(v_one, level, MID_HALO, rows)
    sweep(level, v_ref, 0, v_one, 0, b_ref, 0, 1, total - 1, 6)
    trim(v_ref, level, MID_HALO, rows)
    restrict(
        level, b2_ref, TWO_HALO, two, v_ref, MID_HALO, b_ref, MID_HALO, -2, own + 2, 4
    )
    start(two, w_two, TWO_HALO, b2_ref, TWO_HALO, -2, own + 2, 8)
    trim(w_two, two, TWO_HALO, own)
    sweep(two, v2_ref, TWO_HALO, w_two, TWO_HALO, b2_ref, TWO_HALO, -1, own + 1, 6)
    trim(v2_ref, two, TWO_HALO, own)
    restrict(
        two, b3, 0, three, v2_ref, TWO_HALO, b2_ref, TWO_HALO, 0, own // 2, 2
    )
    even = lane_index() % 2 == 0
    for layer in range(2):
        for pair in range(own // 4):
            row = jnp.where(
                even,
                b3[layer, at(three, 2 * pair), :],
                b3[layer, at(three, 2 * pair + 1), :],
            )
            for copy in range(out_ref.shape[0]):
                out_ref[copy, layer, at(three, pair), :] = row
    up, down = pl.ds((TWO_HALO + 1) * two.size, 3 * two.size), pl.ds(
        own * two.size, 3 * two.size
    )
    up_b, down_b = at(two, TWO_HALO + 2), at(two, TWO_HALO + own - 3)
    last = pl.ds(3 * two.size, two.size)

    tail = pl.ds(4 * two.size, fine.size)
    up_0 = pl.ds((HALO + 1) * fine.size, fine.size)
    down_0 = pl.ds((HALO + 2 * rows - 2) * fine.size, fine.size)

    def send(ref, rows_v, row_b, row_0):
        ref[:, 0 : 3 * two.size, :] = v2_ref[:, rows_v, :]
        ref[:, last, :] = b2_ref[:, row_b, :]
        ref[:, tail, :] = v0_ref[:, row_0, :]

    @pl.when(odd == 1)
    def _():
        send(two_near_ref, up, up_b, up_0)
        send(two_far_ref, down, down_b, down_0)

    @pl.when(odd == 0)
    def _():
        send(two_near_ref, down, down_b, down_0)
        send(two_far_ref, up, up_b, up_0)


PAD = 4


def coarse_solve(level, dst, dst_at, b_ref, n):
    groups = level.stride
    m = n // groups
    part = lane_index() % groups
    source = []
    for layer in range(2):
        source.append([])
        for k in range(m):
            tile = load(b_ref, level, layer, k)[0]
            for g in range(1, groups):
                tile = jnp.where(part == g, load(b_ref, level, layer, g * m + k)[0], tile)
            source[layer].append(level.src[layer] * tile)
    values = source
    for _ in range(COARSE_SWEEPS - 1):
        new = []
        for layer in range(2):
            v, o = values[layer], values[1 - layer]
            below = jnp.where(part == groups - 1, 0.0, pltpu.roll(v[0], LANES - 1, 1))
            above = jnp.where(part == 0, 0.0, pltpu.roll(v[-1], 1, 1))
            out = []
            for k in range(m):
                n_row = v[k + 1] if k + 1 < m else below
                s_row = v[k - 1] if k else above
                e, w = east([v[k]], groups)[0], west([v[k]], groups)[0]
                out.append(
                    (level.keep * v[k] + level.near[layer] * ((n_row + s_row) + (e + w)))
                    + (level.other[layer] * o[k] + source[layer][k])
                )
            new.append(out)
        values = new
    for layer in range(2):
        for k in range(m):
            moved = {
                d: pltpu.roll(values[layer][k], d % LANES, 1) if d else values[layer][k]
                for d in range(1 - groups, groups)
            }
            for g in range(groups):
                tile = moved[-g]
                for j in range(1, groups):
                    tile = jnp.where(part == j, moved[j - g], tile)
                dst[layer, at(level, dst_at + g * m + k), :] = tile


def coarse_kernel(
    levels, rows, same_ref, other_ref, near_ref, far_ref,
    b2_ref, v2_ref, b1_ref, v1_ref, b0_ref, v0_in, out_ref, v0_ref,
    b2, v2, x2, y2, b3, v3, w3, b4, v4, x1, y1, x0, y0, native, sems,
):
    me, odd, is_first, is_last = place()
    fine, mid, two, three, four = levels
    own = rows // 4
    chips = same_ref.shape[0]
    n3, n4 = chips * own, chips * own // 2
    for ref, level, n in ((b3, three, n3), (v3, three, n3), (w3, three, n3), (v4, four, n4)):
        clear(ref, level, 0, PAD)
        clear(ref, level, PAD + n, 2 * PAD + n)
    even = lane_index() % 2 == 0

    def gather_body(chip, carry):
        for ref, core in ((same_ref, odd), (other_ref, 1 - odd)):
            row = (2 * chip + core) * (own // 2) + PAD
            for layer in range(2):
                for pair in range(own // 4):
                    both = ref[chip, layer, at(three, pair), :]
                    first = jnp.where(even, both, pltpu.roll(both, 1, 1))
                    second = jnp.where(even, pltpu.roll(both, LANES - 1, 1), both)
                    b3[layer, at(three, row + 2 * pair), :] = first
                    b3[layer, at(three, row + 2 * pair + 1), :] = second
        return carry

    lax.fori_loop(0, chips, gather_body, 0, unroll=min(chips, 8))

    b2[...] = b2_ref[...]
    v2[...] = v2_ref[...]

    def take(ref, zero):
        top_v, low_v = pl.ds(0, 3 * two.size), pl.ds((TWO_HALO + own + 1) * two.size, 3 * two.size)
        top_b, low_b = at(two, TWO_HALO - 3), at(two, TWO_HALO + own + 2)
        last = pl.ds(3 * two.size, two.size)

        tail = pl.ds(4 * two.size, fine.size)
        top_0 = pl.ds((HALO - 2) * fine.size, fine.size)
        low_0 = pl.ds((HALO + rows + 1) * fine.size, fine.size)

        def drop(values):
            return values if zero is None else jnp.where(zero, 0.0, values)

        def put(rows_v, row_b, row_0):
            v2[:, rows_v, :] = drop(ref[:, 0 : 3 * two.size, :])
            b2[:, row_b, :] = ref[:, last, :]
            v0_ref[:, row_0, :] = drop(ref[:, tail, :])

        return lambda: put(top_v, top_b, top_0), lambda: put(low_v, low_b, low_0)

    near_top, near_low = take(near_ref, None)
    far_top, far_low = take(far_ref, jnp.logical_or(is_first, is_last))

    @pl.when(odd == 1)
    def _():
        near_top()
        far_low()

    @pl.when(odd == 0)
    def _():
        near_low()
        far_top()

    start(three, v3, PAD, b3, PAD, 0, n3, 8)
    sweep(three, w3, PAD, v3, PAD, b3, PAD, 0, n3, 16)
    restrict(three, b4, 0, four, w3, PAD, b3, PAD, 0, n4, 8)
    coarse_solve(four, v4, PAD, b4, n4)

    def trim(ref, level, n):
        @pl.when(me < 2)
        def _():
            clear(ref, level, 0, PAD)

        @pl.when(me >= 2 * chips - 2)
        def _():
            clear(ref, level, PAD + n, 2 * PAD + n)

    half, quarter = own // 2, own // 4
    correct(three, four, v3, PAD, w3, PAD, v4, PAD, me * quarter - 2, quarter + 4, 8)
    sweep(three, w3, PAD, v3, PAD, b3, PAD, me * half - 3, half + 6, 8)
    trim(w3, three, n3)
    sweep(three, v3, PAD, w3, PAD, b3, PAD, me * half - 2, half + 4, 8)
    trim(v3, three, n3)

    def trim_own(ref, level, halo, n):
        @pl.when(is_first)
        def _():
            clear(ref, level, 0, halo)

        @pl.when(is_last)
        def _():
            clear(ref, level, halo + n, 2 * halo + n)

    total = own + 2 * TWO_HALO
    correct(two, three, x2, 0, v2, 0, v3, PAD + me * half - TWO_HALO // 2, 0, total // 2, 8)
    sweep(two, y2, 0, x2, 0, b2, 0, 1, total - 1, 10)
    trim_own(y2, two, TWO_HALO, own)
    sweep(two, x2, 0, y2, 0, b2, 0, 2, total - 2, 8)
    trim_own(x2, two, TWO_HALO, own)

    n1 = rows // 2
    total = n1 + 2 * MID_HALO

    correct(
        mid, two, x1, MID_HALO - 4, v1_ref, MID_HALO - 4, x2, TWO_HALO - 2, 0, n1 // 2 + 4, 4
    )
    sweep(mid, y1, 0, x1, 0, b1_ref, 0, MID_HALO - 2, MID_HALO + n1 + 2, 6)
    trim_own(y1, mid, MID_HALO, n1)
    sweep(mid, x1, 0, y1, 0, b1_ref, 0, MID_HALO - 1, MID_HALO + n1 + 1, 5)
    trim_own(x1, mid, MID_HALO, n1)

    low, high = HALO, HALO + rows
    correct(fine, mid, x0, HALO - 2, v0_ref, HALO - 2, x1, MID_HALO - 1, 0, n1 + 2, 2)
    sweep(fine, y0, 0, x0, 0, b0_ref, 0, low - 1, high + 1, 4)
    trim_own(y0, fine, HALO, rows)
    copies = []
    for group in range(rows // SUBS):
        first_row = low + group * SUBS
        rows_of = pl.ds(group * SUBS, SUBS)
        sweep(fine, x0, 0, y0, 0, b0_ref, 0, first_row, first_row + SUBS, 4)
        for layer in range(2):
            to_native(fine, native, group * SUBS, x0, layer, first_row)
            copies.append(
                pltpu.make_async_copy(
                    native.at[layer, rows_of], out_ref.at[layer, rows_of],
                    sems.at[layer, group],
                )
            )
            copies[-1].start()
    for copy in copies:
        copy.wait()


def shape(*dims):
    return jax.ShapeDtypeStruct(dims, jnp.float32)


def scratch(layers, rows, level):
    return pltpu.VMEM((layers, rows * level.size, LANES), jnp.float32)


HBM = pl.BlockSpec(memory_space=pltpu.HBM)
VMEM = pl.BlockSpec(memory_space=pltpu.VMEM)


def call(kernel, out_shape, scratch_shapes=(), cost=None, limit=24, **options):
    if cost is not None:
        cost = pl.CostEstimate(flops=cost, bytes_accessed=cost // 8, transcendentals=0)
    return pl.pallas_call(
        kernel,
        out_shape=out_shape,
        scratch_shapes=list(scratch_shapes),
        cost_estimate=cost,
        compiler_params=pltpu.CompilerParams(vmem_limit_bytes=limit * 1024 * 1024),
        **options,
    )


def shards(stream_now, vorticity):
    _, rows, columns = stream_now.shape
    count = lax.axis_size("wide")
    tiles = columns // (SUBS * LANES)
    fine, mid = Level(0, tiles, 1), Level(1, tiles // 2, 1)
    two, three, four = Level(2, tiles // 4, 1), Level(3, tiles // 4, 2), Level(4, tiles // 4, 4)
    core_swap = [(i, i ^ 1) for i in range(count)]
    members = lax.axis_size("member")
    inside = [(i, ((i + 1) ^ 1) - 1) for i in range(1, count - 1)]
    if members % 2:
        ends = [(0, count - 1), (count - 1, 0)]
        chip_swap = [(m * count + i, m * count + j) for m in range(members) for i, j in ends]
    else:
        chip_swap = [
            (m * count + i, (m ^ 1) * count + i) for m in range(members) for i in (0, count - 1)
        ]
    chip_swap += [(m * count + i, m * count + j) for m in range(members) for i, j in inside]
    groups = rows // SUBS

    def exchange(near, far):
        far = lax.ppermute(far, ("member", "wide"), chip_swap)
        near = lax.ppermute(near, "wide", core_swap)
        return near, far

    half, quarter = rows // 2, rows // 4
    total = rows + 2 * HALO
    ext, near, far = call(
        functools.partial(pack_kernel, fine, rows),
        [shape(4, total * fine.size, LANES)] + [shape(4, HALO * fine.size, LANES)] * 2,
        [pltpu.VMEM((4, rows, columns), jnp.float32), pltpu.SemaphoreType.DMA((4,))],
        in_specs=[HBM, HBM],
    )(*(pltpu.with_memory_space_constraint(x, pltpu.HBM) for x in (stream_now, vorticity)))
    near, far = exchange(near, far)
    state = [
        shape(4, total * fine.size, LANES),
        shape(4, total * fine.size, LANES),
        shape(2, total * fine.size, LANES),
        shape(2, total * fine.size, LANES),
        shape(2, total * fine.size, LANES),
        shape(2, half * mid.size, LANES),
    ]
    inner = call(
        functools.partial(inner_kernel, fine, mid, rows),
        state,
        cost=8000000,
    )(ext)
    edge = shape(2, MID_HALO * mid.size, LANES)
    outer = call(
        functools.partial(outer_kernel, fine, mid, rows),
        [shape(4, total * fine.size, LANES)] + state + [edge, edge],
        input_output_aliases={i: i for i in range(7)},
    )(ext, *inner, near, far)
    b0, v0, b1, near, far = outer[3], outer[5], outer[6], outer[7], outer[8]
    near, far = exchange(near, far)
    vorticity_next = call(
        functools.partial(emit_kernel, fine, rows),
        shape(2, rows, columns),
        [pltpu.VMEM((2, rows, columns), jnp.float32), pltpu.SemaphoreType.DMA((2, groups))],
        cost=4000000,
        out_specs=HBM,
    )(b0)
    chips = count // 2
    eighth = rows // 8
    two_edge = shape(2, 4 * two.size + fine.size, LANES)
    two_all = shape(2, (quarter + 2 * TWO_HALO) * two.size, LANES)
    b1, v1, b2, v2, b3, near, far = call(
        functools.partial(middle_kernel, fine, mid, two, three, half),
        [
            shape(2, (half + 2 * MID_HALO) * mid.size, LANES),
            shape(2, (half + 2 * MID_HALO) * mid.size, LANES),
            two_all,
            two_all,
            shape(chips, 2, eighth // 2 * three.size, LANES),
            two_edge,
            two_edge,
        ],
        [
            scratch(2, half + 2 * MID_HALO, mid),
            scratch(2, quarter + 2 * TWO_HALO, two),
            scratch(2, eighth, three),
        ],
    )(b1, near, far, v0)
    near, far = exchange(near, far)
    cores = [[i for i in range(count) if i % 2 == c] for c in range(2)]
    same = lax.all_to_all(b3, "wide", 0, 0, axis_index_groups=cores)
    other = lax.ppermute(same, "wide", core_swap)
    n3, n4 = count * eighth, count * eighth // 2
    stream_next, _ = call(
        functools.partial(coarse_kernel, (fine, mid, two, three, four), rows),
        [shape(2, rows, columns), shape(2, total * fine.size, LANES)],
        [scratch(2, quarter + 2 * TWO_HALO, two)] * 4
        + [scratch(2, n3 + 2 * PAD, three)] * 3
        + [scratch(2, n4, four)]
        + [scratch(2, n4 + 2 * PAD, four)]
        + [scratch(2, half + 2 * MID_HALO, mid)] * 2
        + [scratch(2, total, fine)] * 2
        + [pltpu.VMEM((2, rows, columns), jnp.float32), pltpu.SemaphoreType.DMA((2, groups))],
        out_specs=[HBM, VMEM],
        input_output_aliases={9: 1},
    )(same, other, near, far, b2, v2, b1, v1, b0, v0)
    return (vorticity_next, stream_next)


def solution(mesh):
    return jax.shard_map(
        shards,
        mesh=mesh,
        in_specs=(P("member", "wide", None), P("member", "wide", None)),
        out_specs=(P("member", "wide", None), P("member", "wide", None)),
        check_vma=False,
    )
```

profile of v0, /device:TPU:0, one launch (start us, length us, event | category | flops | bytes accessed | tf_op | source)
XLA Modules:
  0.0 37.9 jit_solution(15941571367719173969)
XLA Ops:
  0.6 1.3 %shard_map.41 = (f32[4,704,128]{2,1,0:T(8,128)S(1)}, f32[4,96,128]{2,1,0:T(8,128)S(1)}, f32[4,96,128]{2,1,0:T(8,128)S(1)}) custom-call(f32[2,16,4096]{2,1,0:T(8,128)} %p_ref.1, f32[2,16,4096]{2,1,0:T(8,128)} %q_ref.1), custom_call_target="tpu_custom_call" | custom-call | tf_op jit(solution)/shard_map/pallas_call | solution.py:714
  2.0 0.6 %collective-permute-start = (f32[4,96,128]{2,1,0:T(8,128)S(1)}, f32[4,96,128]{2,1,0:T(8,128)S(1)}, u32[]{:S(2)}, u32[]{:S(2)}) collective-permute-start(f32[4,96,128]{2,1,0:T(8,128)S(1)} %get-tuple-element.31), channel_id=1, source_target_pairs={{0,1},{1,0},{2,3},{3,2},{4,5},{5,4},{6,7},{7,6},{8,9},{9,8},{10,11... | collective-permute-start | bytes 589832 | tf_op jit(solution)/shard_map/ppermute | solution.py:709
  2.5 2.6 %collective-permute-start.1 = (f32[4,96,128]{2,1,0:T(8,128)S(1)}, f32[4,96,128]{2,1,0:T(8,128)S(1)}, u32[]{:S(2)}, u32[]{:S(2)}) collective-permute-start(f32[4,96,128]{2,1,0:T(8,128)S(1)} %get-tuple-element.32), channel_id=1, source_target_pairs={{0,16},{15,31},{16,0},{31,15},{1,2},{2,1},{3,4},{4,3},{5,6},{6,5},... | collective-permute-start | bytes 589832 | tf_op jit(solution)/shard_map/ppermute | solution.py:708
  5.1 2.8 %shard_map.42 = (f32[4,704,128]{2,1,0:T(8,128)S(1)}, f32[4,704,128]{2,1,0:T(8,128)S(1)}, f32[2,704,128]{2,1,0:T(8,128)S(1)}, f32[2,704,128]{2,1,0:T(8,128)S(1)},...) custom-call(f32[4,704,128]{2,1,0:T(8,128)S(1)} %get-tuple-element.24.ext.refs_0_), custom_call_target="tpu_custom_call" | custom-call | flops 8000000 | bytes 1000000 | tf_op jit(solution)/shard_map/pallas_call | solution.py:729
  7.9 0.0 collective-permute-done.refs_7_
  7.9 0.8 %collective-permute-done.1.refs_8_ = f32[4,96,128]{2,1,0:T(8,128)S(1)} collective-permute-done((f32[4,96,128]{2,1,0:T(8,128)S(1)}, f32[4,96,128]{2,1,0:T(8,128)S(1)}, u32[]{:S(2)}, u32[]{:S(2)}) %collective-permute-start.1) | collective-permute-done | bytes 196640 | tf_op jit(solution)/shard_map/ppermute | solution.py:708
  8.7 1.3 %shard_map.43 = (f32[4,704,128]{2,1,0:T(8,128)S(1)}, f32[4,704,128]{2,1,0:T(8,128)S(1)}, f32[4,704,128]{2,1,0:T(8,128)S(1)}, f32[2,704,128]{2,1,0:T(8,128)S(1)},...) custom-call(f32[4,704,128]{2,1,0:T(8,128)S(1)} %get-tuple-element.24, ...), custom_call_target="tpu_custom_call", output_to_operand_aliasing={{0}: (0, {}), {1}: (1, {}), {2}: (2, {}), {3}: (3, {}), {4}... | custom-call | tf_op jit(solution)/shard_map/pallas_call | solution.py:735
  10.0 1.3 %collective-permute-start.2 = (f32[2,96,128]{2,1,0:T(8,128)S(1)}, f32[2,96,128]{2,1,0:T(8,128)S(1)}, u32[]{:S(2)}, u32[]{:S(2)}) collective-permute-start(f32[2,96,128]{2,1,0:T(8,128)S(1)} %get-tuple-element.35), channel_id=1, source_target_pairs={{0,1},{1,0},{2,3},{3,2},{4,5},{5,4},{6,7},{7,6},{8,9},{9,8},{10,11... | collective-permute-start | bytes 294920 | tf_op jit(solution)/shard_map/ppermute | solution.py:709
  11.3 1.5 %collective-permute-start.3 = (f32[2,96,128]{2,1,0:T(8,128)S(1)}, f32[2,96,128]{2,1,0:T(8,128)S(1)}, u32[]{:S(2)}, u32[]{:S(2)}) collective-permute-start(f32[2,96,128]{2,1,0:T(8,128)S(1)} %get-tuple-element.36), channel_id=1, source_target_pairs={{0,16},{15,31},{16,0},{31,15},{1,2},{2,1},{3,4},{4,3},{5,6},{6,5},... | collective-permute-start | bytes 294920 | tf_op jit(solution)/shard_map/ppermute | solution.py:708
  12.8 0.0 collective-permute-done.2.near_ref
  12.8 3.1 %collective-permute-done.3.far_ref = f32[2,96,128]{2,1,0:T(8,128)S(1)} collective-permute-done((f32[2,96,128]{2,1,0:T(8,128)S(1)}, f32[2,96,128]{2,1,0:T(8,128)S(1)}, u32[]{:S(2)}, u32[]{:S(2)}) %collective-permute-start.3) | collective-permute-done | bytes 98336 | tf_op jit(solution)/shard_map/ppermute | solution.py:708
  15.9 2.0 %shard_map.45 = (f32[2,320,128]{2,1,0:T(8,128)S(1)}, f32[2,320,128]{2,1,0:T(8,128)S(1)}, f32[2,96,128]{2,1,0:T(8,128)S(1)}, f32[2,96,128]{2,1,0:T(8,128)S(1)}, f...) custom-call(f32[2,128,128]{2,1,0:T(8,128)S(1)} %get-tuple-element.34.b_own, ...), custom_call_target="tpu_custom_call" | custom-call | tf_op jit(solution)/shard_map/pallas_call | solution.py:753
  17.8 6.6 %all-to-all-start = ((f32[8,2,8,128]{3,2,1,0:T(8,128)}), f32[8,2,8,128]{3,2,1,0:T(8,128)S(1)}, u32[]{:S(2)}, u32[]{:S(2)}) async-start(f32[8,2,8,128]{3,2,1,0:T(8,128)} %get-tuple-element.38), calls=%async_computation | async-start | bytes 131072 | tf_op jit(solution)/shard_map/all_to_all | solution.py:772
  24.4 0.0 collective-permute-start.5
  24.4 1.6 %collective-permute-start.6 = (f32[2,64,128]{2,1,0:T(8,128)S(1)}, f32[2,64,128]{2,1,0:T(8,128)S(1)}, u32[]{:S(2)}, u32[]{:S(2)}) collective-permute-start(f32[2,64,128]{2,1,0:T(8,128)S(1)} %get-tuple-element.40), channel_id=1, source_target_pairs={{0,16},{15,31},{16,0},{31,15},{1,2},{2,1},{3,4},{4,3},{5,6},{6,5},... | collective-permute-start | bytes 196616 | tf_op jit(solution)/shard_map/ppermute | solution.py:708
  26.0 5.3 %all-to-all-done.same_ref = f32[8,2,8,128]{3,2,1,0:T(8,128)S(1)} async-done(((f32[8,2,8,128]{3,2,1,0:T(8,128)}), f32[8,2,8,128]{3,2,1,0:T(8,128)S(1)}, u32[]{:S(2)}, u32[]{:S(2)}) %all-to-all-start) | async-done | bytes 65568 | tf_op jit(solution)/shard_map/all_to_all | solution.py:772
  31.3 0.0 collective-permute-start.4
  31.3 0.9 %shard_map.44 = f32[2,16,4096]{2,1,0:T(8,128)} custom-call(f32[2,704,128]{2,1,0:T(8,128)S(1)} %get-tuple-element.33.b_ref.b0_ref), custom_call_target="tpu_custom_call" | custom-call | flops 4000000 | bytes 500000 | tf_op jit(solution)/shard_map/pallas_call | solution.py:742
  32.2 0.0 collective-permute-done.5.near_ref
  32.2 0.0 collective-permute-done.6.far_ref
  32.2 0.4 collective-permute-done.4.other_ref
  32.6 5.3 %shard_map.46 = (f32[2,16,4096]{2,1,0:T(8,128)}, f32[2,704,128]{2,1,0:T(8,128)S(1)}) custom-call(f32[8,2,8,128]{3,2,1,0:T(8,128)S(1)} %all-to-all-done.same_ref, f32[8,2,8,128]{3,2,1,0:T(8,128)S(1)} %collective-permute-done.4.other_ref, f32[2,64,128]{2,1,0:T(8,128)S(1)} %collective-permute-done.5.near_ref, ...), custom_call_target="tpu_custom_call", output_to_operand_aliasing={{1}: (9, {})} | custom-call | tf_op jit(solution)/shard_map/pallas_call | solution.py:775
Async XLA Ops:
  2.0 5.9 %collective-permute-start = (f32[4,96,128]{2,1,0:T(8,128)S(1)}, f32[4,96,128]{2,1,0:T(8,128)S(1)}, u32[]{:S(2)}, u32[]{:S(2)}) collective-permute-start(f32[4,96,128]{2,1,0:T(8,128)S(1)} %get-tuple-element.31), channel_id=1, source_target_pairs={{0,1},{1,0},{2,3},{3,2},{4,5},{5,4},{6,7},{7,6},{8,9},{9,8},{10,11... | collective-permute-start | bytes 589832 | tf_op jit(solution)/shard_map/ppermute | solution.py:709
  2.5 6.2 %collective-permute-start.1 = (f32[4,96,128]{2,1,0:T(8,128)S(1)}, f32[4,96,128]{2,1,0:T(8,128)S(1)}, u32[]{:S(2)}, u32[]{:S(2)}) collective-permute-start(f32[4,96,128]{2,1,0:T(8,128)S(1)} %get-tuple-element.32), channel_id=1, source_target_pairs={{0,16},{15,31},{16,0},{31,15},{1,2},{2,1},{3,4},{4,3},{5,6},{6,5},... | collective-permute-start | bytes 589832 | tf_op jit(solution)/shard_map/ppermute | solution.py:708
  10.0 2.8 %collective-permute-start.2 = (f32[2,96,128]{2,1,0:T(8,128)S(1)}, f32[2,96,128]{2,1,0:T(8,128)S(1)}, u32[]{:S(2)}, u32[]{:S(2)}) collective-permute-start(f32[2,96,128]{2,1,0:T(8,128)S(1)} %get-tuple-element.35), channel_id=1, source_target_pairs={{0,1},{1,0},{2,3},{3,2},{4,5},{5,4},{6,7},{7,6},{8,9},{9,8},{10,11... | collective-permute-start | bytes 294920 | tf_op jit(solution)/shard_map/ppermute | solution.py:709
  11.3 4.6 %collective-permute-start.3 = (f32[2,96,128]{2,1,0:T(8,128)S(1)}, f32[2,96,128]{2,1,0:T(8,128)S(1)}, u32[]{:S(2)}, u32[]{:S(2)}) collective-permute-start(f32[2,96,128]{2,1,0:T(8,128)S(1)} %get-tuple-element.36), channel_id=1, source_target_pairs={{0,16},{15,31},{16,0},{31,15},{1,2},{2,1},{3,4},{4,3},{5,6},{6,5},... | collective-permute-start | bytes 294920 | tf_op jit(solution)/shard_map/ppermute | solution.py:708
  17.8 13.5 %all-to-all-start = ((f32[8,2,8,128]{3,2,1,0:T(8,128)}), f32[8,2,8,128]{3,2,1,0:T(8,128)S(1)}, u32[]{:S(2)}, u32[]{:S(2)}) async-start(f32[8,2,8,128]{3,2,1,0:T(8,128)} %get-tuple-element.38), calls=%async_computation | async-start | bytes 131072 | tf_op jit(solution)/shard_map/all_to_all | solution.py:772
  24.4 7.8 %collective-permute-start.5 = (f32[2,64,128]{2,1,0:T(8,128)S(1)}, f32[2,64,128]{2,1,0:T(8,128)S(1)}, u32[]{:S(2)}, u32[]{:S(2)}) collective-permute-start(f32[2,64,128]{2,1,0:T(8,128)S(1)} %get-tuple-element.39), channel_id=1, source_target_pairs={{0,1},{1,0},{2,3},{3,2},{4,5},{5,4},{6,7},{7,6},{8,9},{9,8},{10,11... | collective-permute-start | bytes 196616 | tf_op jit(solution)/shard_map/ppermute | solution.py:709
  24.4 7.8 %collective-permute-start.6 = (f32[2,64,128]{2,1,0:T(8,128)S(1)}, f32[2,64,128]{2,1,0:T(8,128)S(1)}, u32[]{:S(2)}, u32[]{:S(2)}) collective-permute-start(f32[2,64,128]{2,1,0:T(8,128)S(1)} %get-tuple-element.40), channel_id=1, source_target_pairs={{0,16},{15,31},{16,0},{31,15},{1,2},{2,1},{3,4},{4,3},{5,6},{6,5},... | collective-permute-start | bytes 196616 | tf_op jit(solution)/shard_map/ppermute | solution.py:708
  31.3 1.3 %collective-permute-start.4 = (f32[8,2,8,128]{3,2,1,0:T(8,128)S(1)}, f32[8,2,8,128]{3,2,1,0:T(8,128)S(1)}, u32[]{:S(2)}, u32[]{:S(2)}) collective-permute-start(f32[8,2,8,128]{3,2,1,0:T(8,128)S(1)} %all-to-all-done.same_ref), channel_id=1, source_target_pairs={{0,1},{1,0},{2,3},{3,2},{4,5},{5,4},{6,7},{7,6},{8,9},{9,8},{10,11... | collective-permute-start | bytes 196616 | tf_op jit(solution)/shard_map/ppermute | solution.py:773
where the time goes:
time: 38.1 us; the launch traced here: 37.9 us
  starting transfers between devices  14 us (37%)
  Pallas kernels  13.5 us (35%)
  waiting for transfers between devices  9.67 us (25%)
  between operations  0.69 us (2%)
    all_to_all x1, starting transfers between devices, shards(): same = lax.all_to_all(b3, 'wide', 0, 0, axis_index_groups=cores)  6.57 us
    ppermute x3, starting transfers between devices, exchange(): far = lax.ppermute(far, ('member', 'wide'), chip_swap)  5.6 us
    all_to_all x1, waiting for transfers between devices, shards(): same = lax.all_to_all(b3, 'wide', 0, 0, axis_index_groups=cores)  5.34 us
    pallas_call x1, Pallas kernels, shards(): call(functools.partial(coarse_kernel, (fine, mid, two, three, four), rows...  5.29 us
    ppermute x3, waiting for transfers between devices, exchange(): far = lax.ppermute(far, ('member', 'wide'), chip_swap)  3.96 us
    pallas_call x1, Pallas kernels, shards(): call(functools.partial(inner_kernel, fine, mid, rows), state, cost=8000000)  2.8 us
    pallas_call x1, Pallas kernels, shards(): call(functools.partial(middle_kernel, fine, mid, two, three, half), [shap...  1.96 us
    ppermute x3, starting transfers between devices, exchange(): near = lax.ppermute(near, 'wide', core_swap)  1.83 us
  transfers between devices with their start and end apart: 8, of which 4 were waited for; matrix products, arithmetic and copies ran while one was open for 0% of the time, Pallas kernels for 10%

commit v1 on v0

--- a/solution.py
+++ b/solution.py
@@ -526,13 +526,9 @@
                 dst[layer, at(level, dst_at + g * m + k), :] = tile
 
 
-def coarse_kernel(
-    levels, rows, same_ref, other_ref, near_ref, far_ref,
-    b2_ref, v2_ref, b1_ref, v1_ref, b0_ref, v0_in, out_ref, v0_ref,
-    b2, v2, x2, y2, b3, v3, w3, b4, v4, x1, y1, x0, y0, native, sems,
-):
+def coarse_kernel(levels, rows, same_ref, other_ref, out_ref, b3, v3, w3, b4, v4):
     me, odd, is_first, is_last = place()
-    fine, mid, two, three, four = levels
+    three, four = levels
     own = rows // 4
     chips = same_ref.shape[0]
     n3, n4 = chips * own, chips * own // 2
@@ -555,6 +551,44 @@
 
     lax.fori_loop(0, chips, gather_body, 0, unroll=min(chips, 8))
 
+    start(three, v3, PAD, b3, PAD, 0, n3, 8)
+    sweep(three, w3, PAD, v3, PAD, b3, PAD, 0, n3, 16)
+    restrict(three, b4, 0, four, w3, PAD, b3, PAD, 0, n4, 8)
+    coarse_solve(four, v4, PAD, b4, n4)
+
+    def trim(ref, level, n):
+        @pl.when(me < 2)
+        def _():
+            clear(ref, level, 0, PAD)
+
+        @pl.when(me >= 2 * chips - 2)
+        def _():
+            clear(ref, level, PAD + n, 2 * PAD + n)
+
+    half, quarter = own // 2, own // 4
+    correct(three, four, v3, PAD, w3, PAD, v4, PAD, me * quarter - 2, quarter + 4, 8)
+    sweep(three, w3, PAD, v3, PAD, b3, PAD, me * half - 3, half + 6, 8)
+    trim(w3, three, n3)
+    sweep(three, out_ref, 2 - me * half, w3, PAD, b3, PAD, me * half - 2, half + 4, 8)
+
+    @pl.when(is_first)
+    def _():
+        clear(out_ref, three, 0, 2)
+
+    @pl.when(is_last)
+    def _():
+        clear(out_ref, three, half + 2, half + 4)
+
+
+def rise_kernel(
+    levels, rows, v3_ref, near_ref, far_ref,
+    b2_ref, v2_ref, b1_ref, v1_ref, b0_ref, v0_in, out_ref, v0_ref,
+    b2, v2, x2, y2, x1, y1, x0, y0, z0, native, sems,
+):
+    _, odd, is_first, is_last = place()
+    fine, mid, two, three = levels
+    own = rows // 4
+
     b2[...] = b2_ref[...]
     v2[...] = v2_ref[...]
 
@@ -590,27 +624,6 @@
         near_low()
         far_top()
 
-    start(three, v3, PAD, b3, PAD, 0, n3, 8)
-    sweep(three, w3, PAD, v3, PAD, b3, PAD, 0, n3, 16)
-    restrict(three, b4, 0, four, w3, PAD, b3, PAD, 0, n4, 8)
-    coarse_solve(four, v4, PAD, b4, n4)
-
-    def trim(ref, level, n):
-        @pl.when(me < 2)
-        def _():
-            clear(ref, level, 0, PAD)
-
-        @pl.when(me >= 2 * chips - 2)
-        def _():
-            clear(ref, level, PAD + n, 2 * PAD + n)
-
-    half, quarter = own // 2, own // 4
-    correct(three, four, v3, PAD, w3, PAD, v4, PAD, me * quarter - 2, quarter + 4, 8)
-    sweep(three, w3, PAD, v3, PAD, b3, PAD, me * half - 3, half + 6, 8)
-    trim(w3, three, n3)
-    sweep(three, v3, PAD, w3, PAD, b3, PAD, me * half - 2, half + 4, 8)
-    trim(v3, three, n3)
-
     def trim_own(ref, level, halo, n):
         @pl.when(is_first)
         def _():
@@ -621,7 +634,7 @@
             clear(ref, level, halo + n, 2 * halo + n)
 
     total = own + 2 * TWO_HALO
-    correct(two, three, x2, 0, v2, 0, v3, PAD + me * half - TWO_HALO // 2, 0, total // 2, 8)
+    correct(two, three, x2, 0, v2, 0, v3_ref, 0, 0, total // 2, 8)
     sweep(two, y2, 0, x2, 0, b2, 0, 1, total - 1, 10)
     trim_own(y2, two, TWO_HALO, own)
     sweep(two, x2, 0, y2, 0, b2, 0, 2, total - 2, 8)
@@ -638,17 +651,19 @@
     sweep(mid, x1, 0, y1, 0, b1_ref, 0, MID_HALO - 1, MID_HALO + n1 + 1, 5)
     trim_own(x1, mid, MID_HALO, n1)
 
-    low, high = HALO, HALO + rows
-    correct(fine, mid, x0, HALO - 2, v0_ref, HALO - 2, x1, MID_HALO - 1, 0, n1 + 2, 2)
-    sweep(fine, y0, 0, x0, 0, b0_ref, 0, low - 1, high + 1, 4)
-    trim_own(y0, fine, HALO, rows)
+    low, done, swept = HALO, 0, HALO - 1
     copies = []
     for group in range(rows // SUBS):
         first_row = low + group * SUBS
         rows_of = pl.ds(group * SUBS, SUBS)
-        sweep(fine, x0, 0, y0, 0, b0_ref, 0, first_row, first_row + SUBS, 4)
+        ready = SUBS // 2 * (group + 1) + 2
+        correct(fine, mid, x0, HALO - 2, v0_ref, HALO - 2, x1, MID_HALO - 1, done, ready, 2)
+        sweep(fine, y0, 0, x0, 0, b0_ref, 0, swept, first_row + SUBS + 1, 5 - group)
+        trim_own(y0, fine, HALO, rows)
+        done, swept = ready, first_row + SUBS + 1
+        sweep(fine, z0, 0, y0, 0, b0_ref, 0, first_row, first_row + SUBS, 4)
         for layer in range(2):
-            to_native(fine, native, group * SUBS, x0, layer, first_row)
+            to_native(fine, native, group * SUBS, z0, layer, first_row)
             copies.append(
                 pltpu.make_async_copy(
                     native.at[layer, rows_of], out_ref.at[layer, rows_of],
@@ -767,24 +782,28 @@
             scratch(2, eighth, three),
         ],
     )(b1, near, far, v0)
-    near, far = exchange(near, far)
     cores = [[i for i in range(count) if i % 2 == c] for c in range(2)]
     same = lax.all_to_all(b3, "wide", 0, 0, axis_index_groups=cores)
     other = lax.ppermute(same, "wide", core_swap)
+    near, far = exchange(near, far)
     n3, n4 = count * eighth, count * eighth // 2
+    v3 = call(
+        functools.partial(coarse_kernel, (three, four), rows),
+        shape(2, (eighth + 4) * three.size, LANES),
+        [scratch(2, n3 + 2 * PAD, three)] * 3
+        + [scratch(2, n4, four), scratch(2, n4 + 2 * PAD, four)],
+        cost=5000000,
+    )(same, other)
     stream_next, _ = call(
-        functools.partial(coarse_kernel, (fine, mid, two, three, four), rows),
+        functools.partial(rise_kernel, (fine, mid, two, three), rows),
         [shape(2, rows, columns), shape(2, total * fine.size, LANES)],
         [scratch(2, quarter + 2 * TWO_HALO, two)] * 4
-        + [scratch(2, n3 + 2 * PAD, three)] * 3
-        + [scratch(2, n4, four)]
-        + [scratch(2, n4 + 2 * PAD, four)]
         + [scratch(2, half + 2 * MID_HALO, mid)] * 2
-        + [scratch(2, total, fine)] * 2
+        + [scratch(2, total, fine)] * 3
         + [pltpu.VMEM((2, rows, columns), jnp.float32), pltpu.SemaphoreType.DMA((2, groups))],
         out_specs=[HBM, VMEM],
-        input_output_aliases={9: 1},
-    )(same, other, near, far, b2, v2, b1, v1, b0, v0)
+        input_output_aliases={8: 1},
+    )(v3, near, far, b2, v2, b1, v1, b0, v0)
     return (vorticity_next, stream_next)
 
 

time: 38.1 us -> 38.8 us (1.018)
  blocking collectives: 0 us -> 13.3 us
  starting transfers between devices: 14 us -> 7.87 us
  waiting for transfers between devices: 9.67 us -> 3.99 us
  Pallas kernels: 13.5 us -> 12.8 us
    all_to_all x0 -> x1, blocking collectives: none -> 13.3 us  [shards(): same = lax.all_to_all(b3, 'wide', 0, 0, axis_index_groups=cores)]
    all_to_all x1 -> x0, starting transfers between devices: 6.57 us -> none  [shards(): same = lax.all_to_all(b3, 'wide', 0, 0, axis_index_groups=cores)]
    all_to_all x1 -> x0, waiting for transfers between devices: 5.34 us -> none  [shards(): same = lax.all_to_all(b3, 'wide', 0, 0, axis_index_groups=cores)]
    pallas_call x1, Pallas kernels: 1.96 us -> 1.33 us  [shards(): call(functools.partial(middle_kernel, fine, mid, two, three, half), [shap...]
    ppermute x3, starting transfers between devices: 1.83 us -> 2.34 us  [exchange(): near = lax.ppermute(near, 'wide', core_swap)]
    pallas_call x1 -> x2, Pallas kernels: 5.29 us -> 5.25 us  [the longest x1 3.4 us: shards(): call(functools.partial(rise_kernel, (fine, mid, two, three), rows), [shap...]
  transfers between devices with their start and end apart: 8 -> 7, of which waited for: 4 -> 2; matrix products, arithmetic and copies ran while one was open for 0% -> 0% of each run, Pallas kernels for 10% -> 14%
where the time goes in v1:
time: 38.8 us; the launch traced here: 38.7 us
  blocking collectives  13.3 us (34%)
  Pallas kernels  12.8 us (33%)
  starting transfers between devices  7.87 us (20%)
  waiting for transfers between devices  3.99 us (10%)
  between operations  0.7 us (2%)
    all_to_all x1, blocking collectives, shards(): same = lax.all_to_all(b3, 'wide', 0, 0, axis_index_groups=cores)  13.3 us
    ppermute x3, starting transfers between devices, exchange(): far = lax.ppermute(far, ('member', 'wide'), chip_swap)  5.53 us
    ppermute x3, waiting for transfers between devices, exchange(): far = lax.ppermute(far, ('member', 'wide'), chip_swap)  3.98 us
    pallas_call x1, Pallas kernels, shards(): call(functools.partial(rise_kernel, (fine, mid, two, three), rows), [shap...  3.4 us
    pallas_call x1, Pallas kernels, shards(): call(functools.partial(inner_kernel, fine, mid, rows), state, cost=8000000)  2.8 us
    ppermute x3, starting transfers between devices, exchange(): near = lax.ppermute(near, 'wide', core_swap)  2.34 us
    pallas_call x1, Pallas kernels, shards(): call(functools.partial(coarse_kernel, (three, four), rows), shape(2, (eig...  1.86 us
    pallas_call x1, Pallas kernels, shards(): call(functools.partial(middle_kernel, fine, mid, two, three, half), [shap...  1.33 us
  transfers between devices with their start and end apart: 7, of which 2 were waited for; matrix products, arithmetic and copies ran while one was open for 0% of the time, Pallas kernels for 14%

profile of v1, /device:TPU:0, one launch (start us, length us, event | category | flops | bytes accessed | tf_op | source)
XLA Modules:
  0.0 38.7 jit_solution(9180208891047521884)
XLA Ops:
  0.6 1.3 %shard_map.41 = (f32[4,704,128]{2,1,0:T(8,128)S(1)}, f32[4,96,128]{2,1,0:T(8,128)S(1)}, f32[4,96,128]{2,1,0:T(8,128)S(1)}) custom-call(f32[2,16,4096]{2,1,0:T(8,128)} %p_ref.1, f32[2,16,4096]{2,1,0:T(8,128)} %q_ref.1), custom_call_target="tpu_custom_call" | custom-call | tf_op jit(solution)/shard_map/pallas_call | solution.py:729
  2.0 0.6 %collective-permute-start = (f32[4,96,128]{2,1,0:T(8,128)S(1)}, f32[4,96,128]{2,1,0:T(8,128)S(1)}, u32[]{:S(2)}, u32[]{:S(2)}) collective-permute-start(f32[4,96,128]{2,1,0:T(8,128)S(1)} %get-tuple-element.31), channel_id=1, source_target_pairs={{0,1},{1,0},{2,3},{3,2},{4,5},{5,4},{6,7},{7,6},{8,9},{9,8},{10,11... | collective-permute-start | bytes 589832 | tf_op jit(solution)/shard_map/ppermute | solution.py:724
  2.5 2.6 %collective-permute-start.1 = (f32[4,96,128]{2,1,0:T(8,128)S(1)}, f32[4,96,128]{2,1,0:T(8,128)S(1)}, u32[]{:S(2)}, u32[]{:S(2)}) collective-permute-start(f32[4,96,128]{2,1,0:T(8,128)S(1)} %get-tuple-element.32), channel_id=1, source_target_pairs={{0,16},{15,31},{16,0},{31,15},{1,2},{2,1},{3,4},{4,3},{5,6},{6,5},... | collective-permute-start | bytes 589832 | tf_op jit(solution)/shard_map/ppermute | solution.py:723
  5.1 2.8 %shard_map.42 = (f32[4,704,128]{2,1,0:T(8,128)S(1)}, f32[4,704,128]{2,1,0:T(8,128)S(1)}, f32[2,704,128]{2,1,0:T(8,128)S(1)}, f32[2,704,128]{2,1,0:T(8,128)S(1)},...) custom-call(f32[4,704,128]{2,1,0:T(8,128)S(1)} %get-tuple-element.24.ext.refs_0_), custom_call_target="tpu_custom_call" | custom-call | flops 8000000 | bytes 1000000 | tf_op jit(solution)/shard_map/pallas_call | solution.py:744
  7.9 0.0 collective-permute-done.refs_7_
  7.9 0.8 %collective-permute-done.1.refs_8_ = f32[4,96,128]{2,1,0:T(8,128)S(1)} collective-permute-done((f32[4,96,128]{2,1,0:T(8,128)S(1)}, f32[4,96,128]{2,1,0:T(8,128)S(1)}, u32[]{:S(2)}, u32[]{:S(2)}) %collective-permute-start.1) | collective-permute-done | bytes 196640 | tf_op jit(solution)/shard_map/ppermute | solution.py:723
  8.7 1.3 %shard_map.43 = (f32[4,704,128]{2,1,0:T(8,128)S(1)}, f32[4,704,128]{2,1,0:T(8,128)S(1)}, f32[4,704,128]{2,1,0:T(8,128)S(1)}, f32[2,704,128]{2,1,0:T(8,128)S(1)},...) custom-call(f32[4,704,128]{2,1,0:T(8,128)S(1)} %get-tuple-element.24, ...), custom_call_target="tpu_custom_call", output_to_operand_aliasing={{0}: (0, {}), {1}: (1, {}), {2}: (2, {}), {3}: (3, {}), {4}... | custom-call | tf_op jit(solution)/shard_map/pallas_call | solution.py:750
  10.0 1.3 %collective-permute-start.2 = (f32[2,96,128]{2,1,0:T(8,128)S(1)}, f32[2,96,128]{2,1,0:T(8,128)S(1)}, u32[]{:S(2)}, u32[]{:S(2)}) collective-permute-start(f32[2,96,128]{2,1,0:T(8,128)S(1)} %get-tuple-element.35), channel_id=1, source_target_pairs={{0,1},{1,0},{2,3},{3,2},{4,5},{5,4},{6,7},{7,6},{8,9},{9,8},{10,11... | collective-permute-start | bytes 294920 | tf_op jit(solution)/shard_map/ppermute | solution.py:724
  11.3 1.5 %collective-permute-start.3 = (f32[2,96,128]{2,1,0:T(8,128)S(1)}, f32[2,96,128]{2,1,0:T(8,128)S(1)}, u32[]{:S(2)}, u32[]{:S(2)}) collective-permute-start(f32[2,96,128]{2,1,0:T(8,128)S(1)} %get-tuple-element.36), channel_id=1, source_target_pairs={{0,16},{15,31},{16,0},{31,15},{1,2},{2,1},{3,4},{4,3},{5,6},{6,5},... | collective-permute-start | bytes 294920 | tf_op jit(solution)/shard_map/ppermute | solution.py:723
  12.8 0.0 collective-permute-done.2.near_ref
  12.8 3.1 %collective-permute-done.3.far_ref = f32[2,96,128]{2,1,0:T(8,128)S(1)} collective-permute-done((f32[2,96,128]{2,1,0:T(8,128)S(1)}, f32[2,96,128]{2,1,0:T(8,128)S(1)}, u32[]{:S(2)}, u32[]{:S(2)}) %collective-permute-start.3) | collective-permute-done | bytes 98336 | tf_op jit(solution)/shard_map/ppermute | solution.py:723
  15.9 1.3 %shard_map.45 = (f32[2,320,128]{2,1,0:T(8,128)S(1)}, f32[2,320,128]{2,1,0:T(8,128)S(1)}, f32[2,96,128]{2,1,0:T(8,128)S(1)}, f32[2,96,128]{2,1,0:T(8,128)S(1)}, f...) custom-call(f32[2,128,128]{2,1,0:T(8,128)S(1)} %get-tuple-element.34.b_own, ...), custom_call_target="tpu_custom_call" | custom-call | tf_op jit(solution)/shard_map/pallas_call | solution.py:768
  17.2 13.3 %all_to_all.5.same_ref = f32[8,2,8,128]{3,2,1,0:T(8,128)S(1)} all-to-all(f32[8,2,8,128]{3,2,1,0:T(8,128)S(1)} %get-tuple-element.38), channel_id=1, replica_groups={{0,2,4,6,8,10,12,14},{1,3,5,7,9,11,13,15},{16,18,20,22,24,26,28,30},{17..., dimensions={0} | all-to-all | bytes 131072 | tf_op jit(solution)/shard_map/all_to_all | solution.py:786
  30.5 0.0 collective-permute-start.4
  30.5 0.5 %collective-permute-start.5 = (f32[2,64,128]{2,1,0:T(8,128)S(1)}, f32[2,64,128]{2,1,0:T(8,128)S(1)}, u32[]{:S(2)}, u32[]{:S(2)}) collective-permute-start(f32[2,64,128]{2,1,0:T(8,128)S(1)} %get-tuple-element.39), channel_id=1, source_target_pairs={{0,1},{1,0},{2,3},{3,2},{4,5},{5,4},{6,7},{7,6},{8,9},{9,8},{10,11... | collective-permute-start | bytes 196616 | tf_op jit(solution)/shard_map/ppermute | solution.py:724
  31.0 1.5 %collective-permute-start.6 = (f32[2,64,128]{2,1,0:T(8,128)S(1)}, f32[2,64,128]{2,1,0:T(8,128)S(1)}, u32[]{:S(2)}, u32[]{:S(2)}) collective-permute-start(f32[2,64,128]{2,1,0:T(8,128)S(1)} %get-tuple-element.40), channel_id=1, source_target_pairs={{0,16},{15,31},{16,0},{31,15},{1,2},{2,1},{3,4},{4,3},{5,6},{6,5},... | collective-permute-start | bytes 196616 | tf_op jit(solution)/shard_map/ppermute | solution.py:723
  32.5 0.9 %shard_map.44 = f32[2,16,4096]{2,1,0:T(8,128)} custom-call(f32[2,704,128]{2,1,0:T(8,128)S(1)} %get-tuple-element.33.b_ref.b0_ref), custom_call_target="tpu_custom_call" | custom-call | flops 4000000 | bytes 500000 | tf_op jit(solution)/shard_map/pallas_call | solution.py:757
  33.4 0.0 collective-permute-done.4.other_ref
  33.4 1.9 %shard_map.46.v3_ref = f32[2,48,128]{2,1,0:T(8,128)S(1)} custom-call(f32[8,2,8,128]{3,2,1,0:T(8,128)S(1)} %all_to_all.5.same_ref, f32[8,2,8,128]{3,2,1,0:T(8,128)S(1)} %collective-permute-done.4.other_ref), custom_call_target="tpu_custom_call" | custom-call | flops 5000000 | bytes 625000 | tf_op jit(solution)/shard_map/pallas_call | solution.py:790
  35.2 0.0 collective-permute-done.5.near_ref
  35.2 0.0 collective-permute-done.6.far_ref
  35.3 3.4 %shard_map.47 = (f32[2,16,4096]{2,1,0:T(8,128)}, f32[2,704,128]{2,1,0:T(8,128)S(1)}) custom-call(f32[2,48,128]{2,1,0:T(8,128)S(1)} %shard_map.46.v3_ref, f32[2,64,128]{2,1,0:T(8,128)S(1)} %collective-permute-done.5.near_ref, f32[2,64,128]{2,1,0:T(8,128)S(1)} %collective-permute-done.6.far_ref, ...), custom_call_target="tpu_custom_call", output_to_operand_aliasing={{1}: (8, {})} | custom-call | tf_op jit(solution)/shard_map/pallas_call | solution.py:797
Async XLA Ops:
  2.0 5.9 %collective-permute-start = (f32[4,96,128]{2,1,0:T(8,128)S(1)}, f32[4,96,128]{2,1,0:T(8,128)S(1)}, u32[]{:S(2)}, u32[]{:S(2)}) collective-permute-start(f32[4,96,128]{2,1,0:T(8,128)S(1)} %get-tuple-element.31), channel_id=1, source_target_pairs={{0,1},{1,0},{2,3},{3,2},{4,5},{5,4},{6,7},{7,6},{8,9},{9,8},{10,11... | collective-permute-start | bytes 589832 | tf_op jit(solution)/shard_map/ppermute | solution.py:724
  2.5 6.2 %collective-permute-start.1 = (f32[4,96,128]{2,1,0:T(8,128)S(1)}, f32[4,96,128]{2,1,0:T(8,128)S(1)}, u32[]{:S(2)}, u32[]{:S(2)}) collective-permute-start(f32[4,96,128]{2,1,0:T(8,128)S(1)} %get-tuple-element.32), channel_id=1, source_target_pairs={{0,16},{15,31},{16,0},{31,15},{1,2},{2,1},{3,4},{4,3},{5,6},{6,5},... | collective-permute-start | bytes 589832 | tf_op jit(solution)/shard_map/ppermute | solution.py:723
  10.0 2.8 %collective-permute-start.2 = (f32[2,96,128]{2,1,0:T(8,128)S(1)}, f32[2,96,128]{2,1,0:T(8,128)S(1)}, u32[]{:S(2)}, u32[]{:S(2)}) collective-permute-start(f32[2,96,128]{2,1,0:T(8,128)S(1)} %get-tuple-element.35), channel_id=1, source_target_pairs={{0,1},{1,0},{2,3},{3,2},{4,5},{5,4},{6,7},{7,6},{8,9},{9,8},{10,11... | collective-permute-start | bytes 294920 | tf_op jit(solution)/shard_map/ppermute | solution.py:724
  11.3 4.6 %collective-permute-start.3 = (f32[2,96,128]{2,1,0:T(8,128)S(1)}, f32[2,96,128]{2,1,0:T(8,128)S(1)}, u32[]{:S(2)}, u32[]{:S(2)}) collective-permute-start(f32[2,96,128]{2,1,0:T(8,128)S(1)} %get-tuple-element.36), channel_id=1, source_target_pairs={{0,16},{15,31},{16,0},{31,15},{1,2},{2,1},{3,4},{4,3},{5,6},{6,5},... | collective-permute-start | bytes 294920 | tf_op jit(solution)/shard_map/ppermute | solution.py:723
  30.5 2.9 %collective-permute-start.4 = (f32[8,2,8,128]{3,2,1,0:T(8,128)S(1)}, f32[8,2,8,128]{3,2,1,0:T(8,128)S(1)}, u32[]{:S(2)}, u32[]{:S(2)}) collective-permute-start(f32[8,2,8,128]{3,2,1,0:T(8,128)S(1)} %all_to_all.5.same_ref), channel_id=1, source_target_pairs={{0,1},{1,0},{2,3},{3,2},{4,5},{5,4},{6,7},{7,6},{8,9},{9,8},{10,11... | collective-permute-start | bytes 196616 | tf_op jit(solution)/shard_map/ppermute | solution.py:787
  30.5 4.7 %collective-permute-start.5 = (f32[2,64,128]{2,1,0:T(8,128)S(1)}, f32[2,64,128]{2,1,0:T(8,128)S(1)}, u32[]{:S(2)}, u32[]{:S(2)}) collective-permute-start(f32[2,64,128]{2,1,0:T(8,128)S(1)} %get-tuple-element.39), channel_id=1, source_target_pairs={{0,1},{1,0},{2,3},{3,2},{4,5},{5,4},{6,7},{7,6},{8,9},{9,8},{10,11... | collective-permute-start | bytes 196616 | tf_op jit(solution)/shard_map/ppermute | solution.py:724
  31.0 4.3 %collective-permute-start.6 = (f32[2,64,128]{2,1,0:T(8,128)S(1)}, f32[2,64,128]{2,1,0:T(8,128)S(1)}, u32[]{:S(2)}, u32[]{:S(2)}) collective-permute-start(f32[2,64,128]{2,1,0:T(8,128)S(1)} %get-tuple-element.40), channel_id=1, source_target_pairs={{0,16},{15,31},{16,0},{31,15},{1,2},{2,1},{3,4},{4,3},{5,6},{6,5},... | collective-permute-start | bytes 196616 | tf_op jit(solution)/shard_map/ppermute | solution.py:723

commit v2 on v1

--- a/solution.py
+++ b/solution.py
@@ -108,9 +108,12 @@
         body(low + whole * block, count % block)
 
 
-def star(rows, k, layer, level):
+def star(rows, k, layer, level, sides=None):
     centre = rows[k][layer]
-    e, w = east(centre, level.stride), west(centre, level.stride)
+    if sides:
+        e, w = sides[0][k][layer], sides[1][k][layer]
+    else:
+        e, w = east(centre, level.stride), west(centre, level.stride)
     return [
         (n + s) + (a + b)
         for n, s, a, b in zip(rows[k + 1][layer], rows[k - 1][layer], e, w)
@@ -124,12 +127,12 @@
     }
 
 
-def sweep_rows(level, rows, source, count):
+def sweep_rows(level, rows, source, count, sides=None):
     out = {}
     for k in range(count):
         out[k] = []
         for layer in range(2):
-            near = star(rows, k, layer, level)
+            near = star(rows, k, layer, level, sides)
             out[k].append(
                 [
                     (level.keep * c + level.near[layer] * n)
@@ -166,11 +169,15 @@
             store(ref, level, layer, first + k, rows[k][layer])
 
 
-def sweep(level, dst, dst_at, src, src_at, b, b_at, low, high, block):
+def sweep(level, dst, dst_at, src, src_at, b, b_at, low, high, block, shifted=None):
     def body(first, count):
         rows = load_rows(src, level, first + src_at, count)
         source = load_rows(b, level, first + b_at, count, 0)
-        store_rows(dst, level, first + dst_at, sweep_rows(level, rows, source, count), count)
+        sides = None
+        if shifted:
+            sides = [load_rows(ref, level, first + src_at, count, 0) for ref in shifted]
+        out = sweep_rows(level, rows, source, count, sides)
+        store_rows(dst, level, first + dst_at, out, count)
 
     row_blocks(low, high, block, body)
 
@@ -354,7 +361,7 @@
     low, high = HALO, HALO + rows
     shift_rows(level, ext, e_ref, w_ref, low, high, 4)
     advance_rows(level, b_ref, ext, e_ref, w_ref, low + 1, high - 1, 2)
-    sweep(level, v_one, 0, ext, 0, b_ref, 0, low + 2, high - 2, 4)
+    sweep(level, v_one, 0, ext, 0, b_ref, 0, low + 2, high - 2, 4, (e_ref, w_ref))
     sweep(level, v_two, 0, v_one, 0, b_ref, 0, low + 3, high - 3, 4)
     restrict(level, bc_ref, 0, coarse, v_two, HALO, b_ref, HALO, 2, rows // 2 - 2, 2)
 
@@ -370,8 +377,8 @@
     shift_rows(level, ext, e_ref, w_ref, high, total, 3)
     advance_rows(level, b_ref, ext, e_ref, w_ref, 1, low + 1, 3)
     advance_rows(level, b_ref, ext, e_ref, w_ref, high - 1, total - 1, 3)
-    sweep(level, v_one, 0, ext, 0, b_ref, 0, 1, low + 2, 4)
-    sweep(level, v_one, 0, ext, 0, b_ref, 0, high - 2, total - 1, 4)
+    sweep(level, v_one, 0, ext, 0, b_ref, 0, 1, low + 2, 4, (e_ref, w_ref))
+    sweep(level, v_one, 0, ext, 0, b_ref, 0, high - 2, total - 1, 4, (e_ref, w_ref))
 
     def trim(ref):
         @pl.when(is_first)
@@ -392,7 +399,7 @@
     send_edges(coarse, MID_HALO, 0, half, bc_ref, bc_near_ref, bc_far_ref)
 
 
-def emit_kernel(level, rows, b_ref, next_ref, native, sems):
+def emit(level, rows, b_ref, next_ref, native, sems):
     copies = []
     for layer in range(2):
         for group in range(rows // SUBS):
@@ -405,8 +412,7 @@
                 )
             )
             copies[-1].start()
-    for copy in copies:
-        copy.wait()
+    return copies
 
 
 def middle_kernel(
@@ -526,9 +532,13 @@
                 dst[layer, at(level, dst_at + g * m + k), :] = tile
 
 
-def coarse_kernel(levels, rows, same_ref, other_ref, out_ref, b3, v3, w3, b4, v4):
+def coarse_kernel(
+    levels, rows, same_ref, other_ref, b0_ref, out_ref, next_ref,
+    b3, v3, w3, b4, v4, native, sems,
+):
     me, odd, is_first, is_last = place()
-    three, four = levels
+    fine, three, four = levels
+    copies = emit(fine, rows, b0_ref, next_ref, native, sems)
     own = rows // 4
     chips = same_ref.shape[0]
     n3, n4 = chips * own, chips * own // 2
@@ -578,6 +588,9 @@
     @pl.when(is_last)
     def _():
         clear(out_ref, three, half + 2, half + 4)
+
+    for copy in copies:
+        copy.wait()
 
 
 def rise_kernel(
@@ -754,13 +767,6 @@
     )(ext, *inner, near, far)
     b0, v0, b1, near, far = outer[3], outer[5], outer[6], outer[7], outer[8]
     near, far = exchange(near, far)
-    vorticity_next = call(
-        functools.partial(emit_kernel, fine, rows),
-        shape(2, rows, columns),
-        [pltpu.VMEM((2, rows, columns), jnp.float32), pltpu.SemaphoreType.DMA((2, groups))],
-        cost=4000000,
-        out_specs=HBM,
-    )(b0)
     chips = count // 2
     eighth = rows // 8
     two_edge = shape(2, 4 * two.size + fine.size, LANES)
@@ -787,13 +793,15 @@
     other = lax.ppermute(same, "wide", core_swap)
     near, far = exchange(near, far)
     n3, n4 = count * eighth, count * eighth // 2
-    v3 = call(
-        functools.partial(coarse_kernel, (three, four), rows),
-        shape(2, (eighth + 4) * three.size, LANES),
+    v3, vorticity_next = call(
+        functools.partial(coarse_kernel, (fine, three, four), rows),
+        [shape(2, (eighth + 4) * three.size, LANES), shape(2, rows, columns)],
         [scratch(2, n3 + 2 * PAD, three)] * 3
-        + [scratch(2, n4, four), scratch(2, n4 + 2 * PAD, four)],
+        + [scratch(2, n4, four), scratch(2, n4 + 2 * PAD, four)]
+        + [pltpu.VMEM((2, rows, columns), jnp.float32), pltpu.SemaphoreType.DMA((2, groups))],
         cost=5000000,
-    )(same, other)
+        out_specs=[VMEM, HBM],
+    )(same, other, b0)
     stream_next, _ = call(
         functools.partial(rise_kernel, (fine, mid, two, three), rows),
         [shape(2, rows, columns), shape(2, total * fine.size, LANES)],

time: 38.8 us -> 38.8 us (level)
  Pallas kernels: 12.8 us -> 11.7 us
  waiting for transfers between devices: 3.99 us -> 5.03 us
    ppermute x3, waiting for transfers between devices: 3.98 us -> 5.02 us  [exchange(): far = lax.ppermute(far, ('member', 'wide'), chip_swap)]
    pallas_call x2 -> x1, Pallas kernels: 2.71 us -> 1.95 us  [shards(): call(functools.partial(coarse_kernel, (fine, three, four), rows), [shape(...]
  transfers between devices with their start and end apart: 7 -> 7, of which waited for: 2 -> 3; matrix products, arithmetic and copies ran while one was open for 0% -> 0% of each run, Pallas kernels for 14% -> 12%
where the time goes in v2:
time: 38.8 us; the launch traced here: 38.6 us
  blocking collectives  13.3 us (34%)
  Pallas kernels  11.7 us (30%)
  starting transfers between devices  7.87 us (20%)
  waiting for transfers between devices  5.03 us (13%)
  between operations  0.69 us (2%)
    all_to_all x1, blocking collectives, shards(): same = lax.all_to_all(b3, 'wide', 0, 0, axis_index_groups=cores)  13.3 us
    ppermute x3, starting transfers between devices, exchange(): far = lax.ppermute(far, ('member', 'wide'), chip_swap)  5.53 us
    ppermute x3, waiting for transfers between devices, exchange(): far = lax.ppermute(far, ('member', 'wide'), chip_swap)  5.02 us
    pallas_call x1, Pallas kernels, shards(): call(functools.partial(rise_kernel, (fine, mid, two, three), rows), [shap...  3.4 us
    pallas_call x1, Pallas kernels, shards(): call(functools.partial(inner_kernel, fine, mid, rows), state, cost=8000000)  2.53 us
    ppermute x3, starting transfers between devices, exchange(): near = lax.ppermute(near, 'wide', core_swap)  2.34 us
    pallas_call x1, Pallas kernels, shards(): call(functools.partial(coarse_kernel, (fine, three, four), rows), [shape(...  1.95 us
    pallas_call x1, Pallas kernels, shards(): call(functools.partial(middle_kernel, fine, mid, two, three, half), [shap...  1.33 us
  transfers between devices with their start and end apart: 7, of which 3 were waited for; matrix products, arithmetic and copies ran while one was open for 0% of the time, Pallas kernels for 12%

profile of v2, /device:TPU:0, one launch (start us, length us, event | category | flops | bytes accessed | tf_op | source)
XLA Modules:
  0.0 38.6 jit_solution(625388371765903347)
XLA Ops:
  0.6 1.3 %shard_map.41 = (f32[4,704,128]{2,1,0:T(8,128)S(1)}, f32[4,96,128]{2,1,0:T(8,128)S(1)}, f32[4,96,128]{2,1,0:T(8,128)S(1)}) custom-call(f32[2,16,4096]{2,1,0:T(8,128)} %p_ref.1, f32[2,16,4096]{2,1,0:T(8,128)} %q_ref.1), custom_call_target="tpu_custom_call" | custom-call | tf_op jit(solution)/shard_map/pallas_call | solution.py:742
  2.0 0.6 %collective-permute-start = (f32[4,96,128]{2,1,0:T(8,128)S(1)}, f32[4,96,128]{2,1,0:T(8,128)S(1)}, u32[]{:S(2)}, u32[]{:S(2)}) collective-permute-start(f32[4,96,128]{2,1,0:T(8,128)S(1)} %get-tuple-element.33), channel_id=1, source_target_pairs={{0,1},{1,0},{2,3},{3,2},{4,5},{5,4},{6,7},{7,6},{8,9},{9,8},{10,11... | collective-permute-start | bytes 589832 | tf_op jit(solution)/shard_map/ppermute | solution.py:737
  2.5 2.6 %collective-permute-start.1 = (f32[4,96,128]{2,1,0:T(8,128)S(1)}, f32[4,96,128]{2,1,0:T(8,128)S(1)}, u32[]{:S(2)}, u32[]{:S(2)}) collective-permute-start(f32[4,96,128]{2,1,0:T(8,128)S(1)} %get-tuple-element.34), channel_id=1, source_target_pairs={{0,16},{15,31},{16,0},{31,15},{1,2},{2,1},{3,4},{4,3},{5,6},{6,5},... | collective-permute-start | bytes 589832 | tf_op jit(solution)/shard_map/ppermute | solution.py:736
  5.1 2.5 %shard_map.42 = (f32[4,704,128]{2,1,0:T(8,128)S(1)}, f32[4,704,128]{2,1,0:T(8,128)S(1)}, f32[2,704,128]{2,1,0:T(8,128)S(1)}, f32[2,704,128]{2,1,0:T(8,128)S(1)},...) custom-call(f32[4,704,128]{2,1,0:T(8,128)S(1)} %get-tuple-element.26.ext.refs_0_), custom_call_target="tpu_custom_call" | custom-call | flops 8000000 | bytes 1000000 | tf_op jit(solution)/shard_map/pallas_call | solution.py:757
  7.6 0.0 collective-permute-done.refs_7_
  7.6 1.1 %collective-permute-done.1.refs_8_ = f32[4,96,128]{2,1,0:T(8,128)S(1)} collective-permute-done((f32[4,96,128]{2,1,0:T(8,128)S(1)}, f32[4,96,128]{2,1,0:T(8,128)S(1)}, u32[]{:S(2)}, u32[]{:S(2)}) %collective-permute-start.1) | collective-permute-done | bytes 196640 | tf_op jit(solution)/shard_map/ppermute | solution.py:736
  8.7 1.2 %shard_map.43 = (f32[4,704,128]{2,1,0:T(8,128)S(1)}, f32[4,704,128]{2,1,0:T(8,128)S(1)}, f32[4,704,128]{2,1,0:T(8,128)S(1)}, f32[2,704,128]{2,1,0:T(8,128)S(1)},...) custom-call(f32[4,704,128]{2,1,0:T(8,128)S(1)} %get-tuple-element.26, ...), custom_call_target="tpu_custom_call", output_to_operand_aliasing={{0}: (0, {}), {1}: (1, {}), {2}: (2, {}), {3}: (3, {}), {4}... | custom-call | tf_op jit(solution)/shard_map/pallas_call | solution.py:763
  9.9 1.3 %collective-permute-start.2 = (f32[2,96,128]{2,1,0:T(8,128)S(1)}, f32[2,96,128]{2,1,0:T(8,128)S(1)}, u32[]{:S(2)}, u32[]{:S(2)}) collective-permute-start(f32[2,96,128]{2,1,0:T(8,128)S(1)} %get-tuple-element.36), channel_id=1, source_target_pairs={{0,1},{1,0},{2,3},{3,2},{4,5},{5,4},{6,7},{7,6},{8,9},{9,8},{10,11... | collective-permute-start | bytes 294920 | tf_op jit(solution)/shard_map/ppermute | solution.py:737
  11.2 1.5 %collective-permute-start.3 = (f32[2,96,128]{2,1,0:T(8,128)S(1)}, f32[2,96,128]{2,1,0:T(8,128)S(1)}, u32[]{:S(2)}, u32[]{:S(2)}) collective-permute-start(f32[2,96,128]{2,1,0:T(8,128)S(1)} %get-tuple-element.37), channel_id=1, source_target_pairs={{0,16},{15,31},{16,0},{31,15},{1,2},{2,1},{3,4},{4,3},{5,6},{6,5},... | collective-permute-start | bytes 294920 | tf_op jit(solution)/shard_map/ppermute | solution.py:736
  12.7 0.0 collective-permute-done.2.near_ref
  12.7 3.1 %collective-permute-done.3.far_ref = f32[2,96,128]{2,1,0:T(8,128)S(1)} collective-permute-done((f32[2,96,128]{2,1,0:T(8,128)S(1)}, f32[2,96,128]{2,1,0:T(8,128)S(1)}, u32[]{:S(2)}, u32[]{:S(2)}) %collective-permute-start.3) | collective-permute-done | bytes 98336 | tf_op jit(solution)/shard_map/ppermute | solution.py:736
  15.8 1.3 %shard_map.44 = (f32[2,320,128]{2,1,0:T(8,128)S(1)}, f32[2,320,128]{2,1,0:T(8,128)S(1)}, f32[2,96,128]{2,1,0:T(8,128)S(1)}, f32[2,96,128]{2,1,0:T(8,128)S(1)}, f...) custom-call(f32[2,128,128]{2,1,0:T(8,128)S(1)} %get-tuple-element.35.b_own, ...), custom_call_target="tpu_custom_call" | custom-call | tf_op jit(solution)/shard_map/pallas_call | solution.py:774
  17.2 13.3 %all_to_all.5.same_ref = f32[8,2,8,128]{3,2,1,0:T(8,128)S(1)} all-to-all(f32[8,2,8,128]{3,2,1,0:T(8,128)S(1)} %get-tuple-element.39), channel_id=1, replica_groups={{0,2,4,6,8,10,12,14},{1,3,5,7,9,11,13,15},{16,18,20,22,24,26,28,30},{17..., dimensions={0} | all-to-all | bytes 131072 | tf_op jit(solution)/shard_map/all_to_all | solution.py:792
  30.4 0.0 collective-permute-start.4
  30.4 0.5 %collective-permute-start.5 = (f32[2,64,128]{2,1,0:T(8,128)S(1)}, f32[2,64,128]{2,1,0:T(8,128)S(1)}, u32[]{:S(2)}, u32[]{:S(2)}) collective-permute-start(f32[2,64,128]{2,1,0:T(8,128)S(1)} %get-tuple-element.43), channel_id=1, source_target_pairs={{0,1},{1,0},{2,3},{3,2},{4,5},{5,4},{6,7},{7,6},{8,9},{9,8},{10,11... | collective-permute-start | bytes 196616 | tf_op jit(solution)/shard_map/ppermute | solution.py:737
  31.0 1.5 %collective-permute-start.6 = (f32[2,64,128]{2,1,0:T(8,128)S(1)}, f32[2,64,128]{2,1,0:T(8,128)S(1)}, u32[]{:S(2)}, u32[]{:S(2)}) collective-permute-start(f32[2,64,128]{2,1,0:T(8,128)S(1)} %get-tuple-element.44), channel_id=1, source_target_pairs={{0,16},{15,31},{16,0},{31,15},{1,2},{2,1},{3,4},{4,3},{5,6},{6,5},... | collective-permute-start | bytes 196616 | tf_op jit(solution)/shard_map/ppermute | solution.py:736
  32.4 0.0 collective-permute-done.4.other_ref
  32.4 2.0 %shard_map.45 = (f32[2,48,128]{2,1,0:T(8,128)S(1)}, f32[2,16,4096]{2,1,0:T(8,128)}) custom-call(f32[8,2,8,128]{3,2,1,0:T(8,128)S(1)} %all_to_all.5.same_ref, f32[8,2,8,128]{3,2,1,0:T(8,128)S(1)} %collective-permute-done.4.other_ref, f32[2,704,128]{2,1,0:T(8,128)S(1)} %get-tuple-element.40.b0_ref), custom_call_target="tpu_custom_call" | custom-call | flops 5000000 | bytes 625000 | tf_op jit(solution)/shard_map/pallas_call | solution.py:796
  34.4 0.0 collective-permute-done.5.near_ref
  34.4 0.8 %collective-permute-done.6.far_ref = f32[2,64,128]{2,1,0:T(8,128)S(1)} collective-permute-done((f32[2,64,128]{2,1,0:T(8,128)S(1)}, f32[2,64,128]{2,1,0:T(8,128)S(1)}, u32[]{:S(2)}, u32[]{:S(2)}) %collective-permute-start.6) | collective-permute-done | bytes 65568 | tf_op jit(solution)/shard_map/ppermute | solution.py:736
  35.2 3.4 %shard_map.46 = (f32[2,16,4096]{2,1,0:T(8,128)}, f32[2,704,128]{2,1,0:T(8,128)S(1)}) custom-call(f32[2,48,128]{2,1,0:T(8,128)S(1)} %get-tuple-element.42.v3_ref, f32[2,64,128]{2,1,0:T(8,128)S(1)} %collective-permute-done.5.near_ref, f32[2,64,128]{2,1,0:T(8,128)S(1)} %collective-permute-done.6.far_ref, ...), custom_call_target="tpu_custom_call", output_to_operand_aliasing={{1}: (8, {})} | custom-call | tf_op jit(solution)/shard_map/pallas_call | solution.py:805
Async XLA Ops:
  2.0 5.7 %collective-permute-start = (f32[4,96,128]{2,1,0:T(8,128)S(1)}, f32[4,96,128]{2,1,0:T(8,128)S(1)}, u32[]{:S(2)}, u32[]{:S(2)}) collective-permute-start(f32[4,96,128]{2,1,0:T(8,128)S(1)} %get-tuple-element.33), channel_id=1, source_target_pairs={{0,1},{1,0},{2,3},{3,2},{4,5},{5,4},{6,7},{7,6},{8,9},{9,8},{10,11... | collective-permute-start | bytes 589832 | tf_op jit(solution)/shard_map/ppermute | solution.py:737
  2.5 6.2 %collective-permute-start.1 = (f32[4,96,128]{2,1,0:T(8,128)S(1)}, f32[4,96,128]{2,1,0:T(8,128)S(1)}, u32[]{:S(2)}, u32[]{:S(2)}) collective-permute-start(f32[4,96,128]{2,1,0:T(8,128)S(1)} %get-tuple-element.34), channel_id=1, source_target_pairs={{0,16},{15,31},{16,0},{31,15},{1,2},{2,1},{3,4},{4,3},{5,6},{6,5},... | collective-permute-start | bytes 589832 | tf_op jit(solution)/shard_map/ppermute | solution.py:736
  9.9 2.8 %collective-permute-start.2 = (f32[2,96,128]{2,1,0:T(8,128)S(1)}, f32[2,96,128]{2,1,0:T(8,128)S(1)}, u32[]{:S(2)}, u32[]{:S(2)}) collective-permute-start(f32[2,96,128]{2,1,0:T(8,128)S(1)} %get-tuple-element.36), channel_id=1, source_target_pairs={{0,1},{1,0},{2,3},{3,2},{4,5},{5,4},{6,7},{7,6},{8,9},{9,8},{10,11... | collective-permute-start | bytes 294920 | tf_op jit(solution)/shard_map/ppermute | solution.py:737
  11.2 4.6 %collective-permute-start.3 = (f32[2,96,128]{2,1,0:T(8,128)S(1)}, f32[2,96,128]{2,1,0:T(8,128)S(1)}, u32[]{:S(2)}, u32[]{:S(2)}) collective-permute-start(f32[2,96,128]{2,1,0:T(8,128)S(1)} %get-tuple-element.37), channel_id=1, source_target_pairs={{0,16},{15,31},{16,0},{31,15},{1,2},{2,1},{3,4},{4,3},{5,6},{6,5},... | collective-permute-start | bytes 294920 | tf_op jit(solution)/shard_map/ppermute | solution.py:736
  30.4 2.0 %collective-permute-start.4 = (f32[8,2,8,128]{3,2,1,0:T(8,128)S(1)}, f32[8,2,8,128]{3,2,1,0:T(8,128)S(1)}, u32[]{:S(2)}, u32[]{:S(2)}) collective-permute-start(f32[8,2,8,128]{3,2,1,0:T(8,128)S(1)} %all_to_all.5.same_ref), channel_id=1, source_target_pairs={{0,1},{1,0},{2,3},{3,2},{4,5},{5,4},{6,7},{7,6},{8,9},{9,8},{10,11... | collective-permute-start | bytes 196616 | tf_op jit(solution)/shard_map/ppermute | solution.py:793
  30.4 4.0 %collective-permute-start.5 = (f32[2,64,128]{2,1,0:T(8,128)S(1)}, f32[2,64,128]{2,1,0:T(8,128)S(1)}, u32[]{:S(2)}, u32[]{:S(2)}) collective-permute-start(f32[2,64,128]{2,1,0:T(8,128)S(1)} %get-tuple-element.43), channel_id=1, source_target_pairs={{0,1},{1,0},{2,3},{3,2},{4,5},{5,4},{6,7},{7,6},{8,9},{9,8},{10,11... | collective-permute-start | bytes 196616 | tf_op jit(solution)/shard_map/ppermute | solution.py:737
  31.0 4.3 %collective-permute-start.6 = (f32[2,64,128]{2,1,0:T(8,128)S(1)}, f32[2,64,128]{2,1,0:T(8,128)S(1)}, u32[]{:S(2)}, u32[]{:S(2)}) collective-permute-start(f32[2,64,128]{2,1,0:T(8,128)S(1)} %get-tuple-element.44), channel_id=1, source_target_pairs={{0,16},{15,31},{16,0},{31,15},{1,2},{2,1},{3,4},{4,3},{5,6},{6,5},... | collective-permute-start | bytes 196616 | tf_op jit(solution)/shard_map/ppermute | solution.py:736

commit v3 on v2

--- a/solution.py
+++ b/solution.py
@@ -99,6 +99,8 @@
 
 def row_blocks(low, high, block, body):
     count = high - low if isinstance(low, int) else high
+    if count <= 48:
+        block = count
     whole = count // block
     if whole > 1:
         lax.fori_loop(0, whole, lambda i, c: (body(low + i * block, block), c)[1], 0)
@@ -272,26 +274,34 @@
     return me, lax.rem(me, 2), me == 0, me == count - 1
 
 
-def pack_kernel(level, rows, p_ref, q_ref, ext_ref, near_ref, far_ref, native, sems):
+def pack_kernel(level, rows, far, p_ref, q_ref, *refs):
+    ext_ref, edge_ref, native, sems = refs[-4:]
+    _, odd, _, _ = place()
+    at_end = odd == 1 if far else odd == 0
+    count = SUBS if far else rows - SUBS
+    first = pl.multiple_of(jnp.where(at_end, rows - count, 0), SUBS)
     copies = []
     for field, ref in enumerate((p_ref, q_ref)):
         for layer in range(2):
             which = 2 * field + layer
             copies.append(
-                pltpu.make_async_copy(ref.at[layer], native.at[which], sems.at[which])
+                pltpu.make_async_copy(
+                    ref.at[layer, pl.ds(first, count)], native.at[which], sems.at[which]
+                )
             )
             copies[-1].start()
     for which in range(4):
         copies[which].wait()
-        for group in range(rows // SUBS):
+        for group in range(count // SUBS):
             for t in range(level.tiles):
                 tiles = [
                     native[which, group * SUBS : (group + 1) * SUBS, column_of(level, t, s)]
                     for s in range(SUBS)
                 ]
                 for r, tile in enumerate(transpose_tiles(tiles)):
-                    ext_ref[which, at(level, HALO + group * SUBS + r, t), :] = tile
-    send_edges(level, HALO, HALO, rows, ext_ref, near_ref, far_ref)
+                    ext_ref[which, at(level, first + HALO + group * SUBS + r, t), :] = tile
+    edge = jnp.where(at_end, rows, HALO) * level.size
+    edge_ref[...] = ext_ref[:, pl.ds(pl.multiple_of(edge, SUBS), HALO * level.size), :]
 
 
 def send_edges(level, width, src_at, rows, src, near_ref, far_ref):
@@ -739,12 +749,26 @@
 
     half, quarter = rows // 2, rows // 4
     total = rows + 2 * HALO
-    ext, near, far = call(
-        functools.partial(pack_kernel, fine, rows),
-        [shape(4, total * fine.size, LANES)] + [shape(4, HALO * fine.size, LANES)] * 2,
-        [pltpu.VMEM((4, rows, columns), jnp.float32), pltpu.SemaphoreType.DMA((4,))],
-        in_specs=[HBM, HBM],
-    )(*(pltpu.with_memory_space_constraint(x, pltpu.HBM) for x in (stream_now, vorticity)))
+    inputs = [pltpu.with_memory_space_constraint(x, pltpu.HBM) for x in (stream_now, vorticity)]
+
+    def pack(far, packed):
+        return call(
+            functools.partial(pack_kernel, fine, rows, far),
+            [
+                shape(4, total * fine.size, LANES),
+                shape(4, HALO * fine.size, LANES),
+            ],
+            [
+                pltpu.VMEM((4, SUBS if far else rows - SUBS, columns), jnp.float32),
+                pltpu.SemaphoreType.DMA((4,)),
+            ],
+            cost=2000000,
+            in_specs=[HBM, HBM] + [VMEM] * len(packed),
+            input_output_aliases={2: 0} if packed else {},
+        )(*inputs, *packed)
+
+    ext, far = pack(True, [])
+    ext, near = pack(False, [ext])
     near, far = exchange(near, far)
     state = [
         shape(4, total * fine.size, LANES),

time: 38.8 us -> 38.6 us (level)
  Pallas kernels: 11.7 us -> 10.8 us
  waiting for transfers between devices: 5.03 us -> 5.76 us
    pallas_call x1 -> x2, Pallas kernels: 1.32 us -> 2.39 us  [pack(): call(functools.partial(pack_kernel, fine, rows, far), [shape(4, total * f...]
    pallas_call x1, Pallas kernels: 3.4 us -> 2.37 us  [shards(): call(functools.partial(rise_kernel, (fine, mid, two, three), rows), [shap...]
    pallas_call x1, Pallas kernels: 2.53 us -> 1.56 us  [shards(): call(functools.partial(inner_kernel, fine, mid, rows), state, cost=8000000)]
    ppermute x3, waiting for transfers between devices: 5.02 us -> 5.75 us  [exchange(): far = lax.ppermute(far, ('member', 'wide'), chip_swap)]
  transfers between devices with their start and end apart: 7 -> 7, of which waited for: 3 -> 3; matrix products, arithmetic and copies ran while one was open for 0% -> 0% of each run, Pallas kernels for 12% -> 10%
where the time goes in v3:
time: 38.6 us; the launch traced here: 38.4 us
  blocking collectives  13.3 us (34%)
  Pallas kernels  10.8 us (28%)
  starting transfers between devices  7.87 us (20%)
  waiting for transfers between devices  5.76 us (15%)
  between operations  0.69 us (2%)
    all_to_all x1, blocking collectives, shards(): same = lax.all_to_all(b3, 'wide', 0, 0, axis_index_groups=cores)  13.3 us
    ppermute x3, waiting for transfers between devices, exchange(): far = lax.ppermute(far, ('member', 'wide'), chip_swap)  5.75 us
    ppermute x3, starting transfers between devices, exchange(): far = lax.ppermute(far, ('member', 'wide'), chip_swap)  5.53 us
    pallas_call x2, Pallas kernels, pack(): call(functools.partial(pack_kernel, fine, rows, far), [shape(4, total * f...  2.39 us
    pallas_call x1, Pallas kernels, shards(): call(functools.partial(rise_kernel, (fine, mid, two, three), rows), [shap...  2.37 us
    ppermute x3, starting transfers between devices, exchange(): near = lax.ppermute(near, 'wide', core_swap)  2.34 us
    pallas_call x1, Pallas kernels, shards(): call(functools.partial(coarse_kernel, (fine, three, four), rows), [shape(...  2.19 us
    pallas_call x1, Pallas kernels, shards(): call(functools.partial(inner_kernel, fine, mid, rows), state, cost=8000000)  1.56 us
  transfers between devices with their start and end apart: 7, of which 3 were waited for; matrix products, arithmetic and copies ran while one was open for 0% of the time, Pallas kernels for 10%

profile of v3, /device:TPU:0, one launch (start us, length us, event | category | flops | bytes accessed | tf_op | source)
XLA Modules:
  0.0 38.4 jit_solution(9808131790653829419)
XLA Ops:
  0.6 1.2 %shard_map.41 = (f32[4,704,128]{2,1,0:T(8,128)S(1)}, f32[4,96,128]{2,1,0:T(8,128)S(1)}) custom-call(f32[2,16,4096]{2,1,0:T(8,128)} %p_ref.3, f32[2,16,4096]{2,1,0:T(8,128)} %q_ref.3), custom_call_target="tpu_custom_call" | custom-call | flops 2000000 | bytes 250000 | tf_op jit(solution)/shard_map/pallas_call | solution.py:755
  1.8 1.2 %shard_map.42 = (f32[4,704,128]{2,1,0:T(8,128)S(1)}, f32[4,96,128]{2,1,0:T(8,128)S(1)}) custom-call(f32[2,16,4096]{2,1,0:T(8,128)} %p_ref.3, f32[2,16,4096]{2,1,0:T(8,128)} %q_ref.3, f32[4,704,128]{2,1,0:T(8,128)S(1)} %get-tuple-element.27.refs_0_), custom_call_target="tpu_custom_call", output_to_operand_aliasing={{0}: (2, {})} | custom-call | flops 2000000 | bytes 250000 | tf_op jit(solution)/shard_map/pallas_call | solution.py:755
  3.0 0.6 %collective-permute-start = (f32[4,96,128]{2,1,0:T(8,128)S(1)}, f32[4,96,128]{2,1,0:T(8,128)S(1)}, u32[]{:S(2)}, u32[]{:S(2)}) collective-permute-start(f32[4,96,128]{2,1,0:T(8,128)S(1)} %get-tuple-element.35), channel_id=1, source_target_pairs={{0,1},{1,0},{2,3},{3,2},{4,5},{5,4},{6,7},{7,6},{8,9},{9,8},{10,11... | collective-permute-start | bytes 589832 | tf_op jit(solution)/shard_map/ppermute | solution.py:747
  3.6 2.6 %collective-permute-start.1 = (f32[4,96,128]{2,1,0:T(8,128)S(1)}, f32[4,96,128]{2,1,0:T(8,128)S(1)}, u32[]{:S(2)}, u32[]{:S(2)}) collective-permute-start(f32[4,96,128]{2,1,0:T(8,128)S(1)} %get-tuple-element.36), channel_id=1, source_target_pairs={{0,16},{15,31},{16,0},{31,15},{1,2},{2,1},{3,4},{4,3},{5,6},{6,5},... | collective-permute-start | bytes 589832 | tf_op jit(solution)/shard_map/ppermute | solution.py:746
  6.1 1.6 %shard_map.43 = (f32[4,704,128]{2,1,0:T(8,128)S(1)}, f32[4,704,128]{2,1,0:T(8,128)S(1)}, f32[2,704,128]{2,1,0:T(8,128)S(1)}, f32[2,704,128]{2,1,0:T(8,128)S(1)},...) custom-call(f32[4,704,128]{2,1,0:T(8,128)S(1)} %get-tuple-element.28.ext.refs_0_), custom_call_target="tpu_custom_call" | custom-call | flops 8000000 | bytes 1000000 | tf_op jit(solution)/shard_map/pallas_call | solution.py:781
  7.7 0.0 collective-permute-done.refs_7_
  7.7 2.1 %collective-permute-done.1.refs_8_ = f32[4,96,128]{2,1,0:T(8,128)S(1)} collective-permute-done((f32[4,96,128]{2,1,0:T(8,128)S(1)}, f32[4,96,128]{2,1,0:T(8,128)S(1)}, u32[]{:S(2)}, u32[]{:S(2)}) %collective-permute-start.1) | collective-permute-done | bytes 196640 | tf_op jit(solution)/shard_map/ppermute | solution.py:746
  9.8 1.2 %shard_map.44 = (f32[4,704,128]{2,1,0:T(8,128)S(1)}, f32[4,704,128]{2,1,0:T(8,128)S(1)}, f32[4,704,128]{2,1,0:T(8,128)S(1)}, f32[2,704,128]{2,1,0:T(8,128)S(1)},...) custom-call(f32[4,704,128]{2,1,0:T(8,128)S(1)} %get-tuple-element.28, ...), custom_call_target="tpu_custom_call", output_to_operand_aliasing={{0}: (0, {}), {1}: (1, {}), {2}: (2, {}), {3}: (3, {}), {4}... | custom-call | tf_op jit(solution)/shard_map/pallas_call | solution.py:787
  11.0 1.3 %collective-permute-start.2 = (f32[2,96,128]{2,1,0:T(8,128)S(1)}, f32[2,96,128]{2,1,0:T(8,128)S(1)}, u32[]{:S(2)}, u32[]{:S(2)}) collective-permute-start(f32[2,96,128]{2,1,0:T(8,128)S(1)} %get-tuple-element.38), channel_id=1, source_target_pairs={{0,1},{1,0},{2,3},{3,2},{4,5},{5,4},{6,7},{7,6},{8,9},{9,8},{10,11... | collective-permute-start | bytes 294920 | tf_op jit(solution)/shard_map/ppermute | solution.py:747
  12.3 1.5 %collective-permute-start.3 = (f32[2,96,128]{2,1,0:T(8,128)S(1)}, f32[2,96,128]{2,1,0:T(8,128)S(1)}, u32[]{:S(2)}, u32[]{:S(2)}) collective-permute-start(f32[2,96,128]{2,1,0:T(8,128)S(1)} %get-tuple-element.39), channel_id=1, source_target_pairs={{0,16},{15,31},{16,0},{31,15},{1,2},{2,1},{3,4},{4,3},{5,6},{6,5},... | collective-permute-start | bytes 294920 | tf_op jit(solution)/shard_map/ppermute | solution.py:746
  13.8 0.0 collective-permute-done.2.near_ref
  13.8 3.1 %collective-permute-done.3.far_ref = f32[2,96,128]{2,1,0:T(8,128)S(1)} collective-permute-done((f32[2,96,128]{2,1,0:T(8,128)S(1)}, f32[2,96,128]{2,1,0:T(8,128)S(1)}, u32[]{:S(2)}, u32[]{:S(2)}) %collective-permute-start.3) | collective-permute-done | bytes 98336 | tf_op jit(solution)/shard_map/ppermute | solution.py:746
  16.9 1.1 %shard_map.45 = (f32[2,320,128]{2,1,0:T(8,128)S(1)}, f32[2,320,128]{2,1,0:T(8,128)S(1)}, f32[2,96,128]{2,1,0:T(8,128)S(1)}, f32[2,96,128]{2,1,0:T(8,128)S(1)}, f...) custom-call(f32[2,128,128]{2,1,0:T(8,128)S(1)} %get-tuple-element.37.b_own, ...), custom_call_target="tpu_custom_call" | custom-call | tf_op jit(solution)/shard_map/pallas_call | solution.py:798
  18.0 13.3 %all_to_all.5.same_ref = f32[8,2,8,128]{3,2,1,0:T(8,128)S(1)} all-to-all(f32[8,2,8,128]{3,2,1,0:T(8,128)S(1)} %get-tuple-element.41), channel_id=1, replica_groups={{0,2,4,6,8,10,12,14},{1,3,5,7,9,11,13,15},{16,18,20,22,24,26,28,30},{17..., dimensions={0} | all-to-all | bytes 131072 | tf_op jit(solution)/shard_map/all_to_all | solution.py:816
  31.3 0.0 collective-permute-start.4
  31.3 0.5 %collective-permute-start.5 = (f32[2,64,128]{2,1,0:T(8,128)S(1)}, f32[2,64,128]{2,1,0:T(8,128)S(1)}, u32[]{:S(2)}, u32[]{:S(2)}) collective-permute-start(f32[2,64,128]{2,1,0:T(8,128)S(1)} %get-tuple-element.45), channel_id=1, source_target_pairs={{0,1},{1,0},{2,3},{3,2},{4,5},{5,4},{6,7},{7,6},{8,9},{9,8},{10,11... | collective-permute-start | bytes 196616 | tf_op jit(solution)/shard_map/ppermute | solution.py:747
  31.8 1.5 %collective-permute-start.6 = (f32[2,64,128]{2,1,0:T(8,128)S(1)}, f32[2,64,128]{2,1,0:T(8,128)S(1)}, u32[]{:S(2)}, u32[]{:S(2)}) collective-permute-start(f32[2,64,128]{2,1,0:T(8,128)S(1)} %get-tuple-element.46), channel_id=1, source_target_pairs={{0,16},{15,31},{16,0},{31,15},{1,2},{2,1},{3,4},{4,3},{5,6},{6,5},... | collective-permute-start | bytes 196616 | tf_op jit(solution)/shard_map/ppermute | solution.py:746
  33.3 0.0 collective-permute-done.4.other_ref
  33.3 2.2 %shard_map.46 = (f32[2,48,128]{2,1,0:T(8,128)S(1)}, f32[2,16,4096]{2,1,0:T(8,128)}) custom-call(f32[8,2,8,128]{3,2,1,0:T(8,128)S(1)} %all_to_all.5.same_ref, f32[8,2,8,128]{3,2,1,0:T(8,128)S(1)} %collective-permute-done.4.other_ref, f32[2,704,128]{2,1,0:T(8,128)S(1)} %get-tuple-element.42.b0_ref), custom_call_target="tpu_custom_call" | custom-call | flops 5000000 | bytes 625000 | tf_op jit(solution)/shard_map/pallas_call | solution.py:820
  35.5 0.0 collective-permute-done.5.near_ref
  35.5 0.6 %collective-permute-done.6.far_ref = f32[2,64,128]{2,1,0:T(8,128)S(1)} collective-permute-done((f32[2,64,128]{2,1,0:T(8,128)S(1)}, f32[2,64,128]{2,1,0:T(8,128)S(1)}, u32[]{:S(2)}, u32[]{:S(2)}) %collective-permute-start.6) | collective-permute-done | bytes 65568 | tf_op jit(solution)/shard_map/ppermute | solution.py:746
  36.0 2.4 %shard_map.47 = (f32[2,16,4096]{2,1,0:T(8,128)}, f32[2,704,128]{2,1,0:T(8,128)S(1)}) custom-call(f32[2,48,128]{2,1,0:T(8,128)S(1)} %get-tuple-element.44.v3_ref, f32[2,64,128]{2,1,0:T(8,128)S(1)} %collective-permute-done.5.near_ref, f32[2,64,128]{2,1,0:T(8,128)S(1)} %collective-permute-done.6.far_ref, ...), custom_call_target="tpu_custom_call", output_to_operand_aliasing={{1}: (8, {})} | custom-call | tf_op jit(solution)/shard_map/pallas_call | solution.py:829
Async XLA Ops:
  3.0 4.7 %collective-permute-start = (f32[4,96,128]{2,1,0:T(8,128)S(1)}, f32[4,96,128]{2,1,0:T(8,128)S(1)}, u32[]{:S(2)}, u32[]{:S(2)}) collective-permute-start(f32[4,96,128]{2,1,0:T(8,128)S(1)} %get-tuple-element.35), channel_id=1, source_target_pairs={{0,1},{1,0},{2,3},{3,2},{4,5},{5,4},{6,7},{7,6},{8,9},{9,8},{10,11... | collective-permute-start | bytes 589832 | tf_op jit(solution)/shard_map/ppermute | solution.py:747
  3.6 6.2 %collective-permute-start.1 = (f32[4,96,128]{2,1,0:T(8,128)S(1)}, f32[4,96,128]{2,1,0:T(8,128)S(1)}, u32[]{:S(2)}, u32[]{:S(2)}) collective-permute-start(f32[4,96,128]{2,1,0:T(8,128)S(1)} %get-tuple-element.36), channel_id=1, source_target_pairs={{0,16},{15,31},{16,0},{31,15},{1,2},{2,1},{3,4},{4,3},{5,6},{6,5},... | collective-permute-start | bytes 589832 | tf_op jit(solution)/shard_map/ppermute | solution.py:746
  11.0 2.8 %collective-permute-start.2 = (f32[2,96,128]{2,1,0:T(8,128)S(1)}, f32[2,96,128]{2,1,0:T(8,128)S(1)}, u32[]{:S(2)}, u32[]{:S(2)}) collective-permute-start(f32[2,96,128]{2,1,0:T(8,128)S(1)} %get-tuple-element.38), channel_id=1, source_target_pairs={{0,1},{1,0},{2,3},{3,2},{4,5},{5,4},{6,7},{7,6},{8,9},{9,8},{10,11... | collective-permute-start | bytes 294920 | tf_op jit(solution)/shard_map/ppermute | solution.py:747
  12.3 4.6 %collective-permute-start.3 = (f32[2,96,128]{2,1,0:T(8,128)S(1)}, f32[2,96,128]{2,1,0:T(8,128)S(1)}, u32[]{:S(2)}, u32[]{:S(2)}) collective-permute-start(f32[2,96,128]{2,1,0:T(8,128)S(1)} %get-tuple-element.39), channel_id=1, source_target_pairs={{0,16},{15,31},{16,0},{31,15},{1,2},{2,1},{3,4},{4,3},{5,6},{6,5},... | collective-permute-start | bytes 294920 | tf_op jit(solution)/shard_map/ppermute | solution.py:746
  31.3 2.0 %collective-permute-start.4 = (f32[8,2,8,128]{3,2,1,0:T(8,128)S(1)}, f32[8,2,8,128]{3,2,1,0:T(8,128)S(1)}, u32[]{:S(2)}, u32[]{:S(2)}) collective-permute-start(f32[8,2,8,128]{3,2,1,0:T(8,128)S(1)} %all_to_all.5.same_ref), channel_id=1, source_target_pairs={{0,1},{1,0},{2,3},{3,2},{4,5},{5,4},{6,7},{7,6},{8,9},{9,8},{10,11... | collective-permute-start | bytes 196616 | tf_op jit(solution)/shard_map/ppermute | solution.py:817
  31.3 4.2 %collective-permute-start.5 = (f32[2,64,128]{2,1,0:T(8,128)S(1)}, f32[2,64,128]{2,1,0:T(8,128)S(1)}, u32[]{:S(2)}, u32[]{:S(2)}) collective-permute-start(f32[2,64,128]{2,1,0:T(8,128)S(1)} %get-tuple-element.45), channel_id=1, source_target_pairs={{0,1},{1,0},{2,3},{3,2},{4,5},{5,4},{6,7},{7,6},{8,9},{9,8},{10,11... | collective-permute-start | bytes 196616 | tf_op jit(solution)/shard_map/ppermute | solution.py:747
  31.8 4.3 %collective-permute-start.6 = (f32[2,64,128]{2,1,0:T(8,128)S(1)}, f32[2,64,128]{2,1,0:T(8,128)S(1)}, u32[]{:S(2)}, u32[]{:S(2)}) collective-permute-start(f32[2,64,128]{2,1,0:T(8,128)S(1)} %get-tuple-element.46), channel_id=1, source_target_pairs={{0,16},{15,31},{16,0},{31,15},{1,2},{2,1},{3,4},{4,3},{5,6},{6,5},... | collective-permute-start | bytes 196616 | tf_op jit(solution)/shard_map/ppermute | solution.py:746

commit v4 on v2

--- a/solution.py
+++ b/solution.py
@@ -97,8 +97,10 @@
             )
 
 
-def row_blocks(low, high, block, body):
+def row_blocks(low, high, block, body, straight=48):
     count = high - low if isinstance(low, int) else high
+    if count <= straight:
+        block = count
     whole = count // block
     if whole > 1:
         lax.fori_loop(0, whole, lambda i, c: (body(low + i * block, block), c)[1], 0)
@@ -169,7 +171,7 @@
             store(ref, level, layer, first + k, rows[k][layer])
 
 
-def sweep(level, dst, dst_at, src, src_at, b, b_at, low, high, block, shifted=None):
+def sweep(level, dst, dst_at, src, src_at, b, b_at, low, high, block, shifted=None, straight=48):
     def body(first, count):
         rows = load_rows(src, level, first + src_at, count)
         source = load_rows(b, level, first + b_at, count, 0)
@@ -179,7 +181,7 @@
         out = sweep_rows(level, rows, source, count, sides)
         store_rows(dst, level, first + dst_at, out, count)
 
-    row_blocks(low, high, block, body)
+    row_blocks(low, high, block, body, straight)
 
 
 def start(level, dst, dst_at, b, b_at, low, high, block):
@@ -222,7 +224,9 @@
     ]
 
 
-def restrict(fine, dst, dst_at, coarse, src, src_at, b, b_at, low, high, block):
+def restrict(
+    fine, dst, dst_at, coarse, src, src_at, b, b_at, low, high, block, straight=48
+):
     def body(first, count):
         rows = load_rows(src, fine, 2 * first + src_at, 2 * count)
         source = load_rows(b, fine, 2 * first + b_at, 2 * count, 0)
@@ -239,7 +243,7 @@
                 out[k].append([0.25 * x for x in pair])
         store_rows(dst, coarse, first + dst_at, out, count)
 
-    row_blocks(low, high, block, body)
+    row_blocks(low, high, block, body, straight)
 
 
 def correct(fine, coarse, dst, dst_at, src, src_at, add, add_at, low, high, block):
@@ -562,8 +566,8 @@
     lax.fori_loop(0, chips, gather_body, 0, unroll=min(chips, 8))
 
     start(three, v3, PAD, b3, PAD, 0, n3, 8)
-    sweep(three, w3, PAD, v3, PAD, b3, PAD, 0, n3, 16)
-    restrict(three, b4, 0, four, w3, PAD, b3, PAD, 0, n4, 8)
+    sweep(three, w3, PAD, v3, PAD, b3, PAD, 0, n3, 16, straight=0)
+    restrict(three, b4, 0, four, w3, PAD, b3, PAD, 0, n4, 8, straight=0)
     coarse_solve(four, v4, PAD, b4, n4)
 
     def trim(ref, level, n):

time: 38.8 us -> 37.5 us (0.966)
  Pallas kernels: 11.7 us -> 9.53 us
  waiting for transfers between devices: 5.03 us -> 5.97 us
    pallas_call x1, Pallas kernels: 3.4 us -> 2.37 us  [shards(): call(functools.partial(rise_kernel, (fine, mid, two, three), rows), [shap...]
    pallas_call x1, Pallas kernels: 2.53 us -> 1.56 us  [shards(): call(functools.partial(inner_kernel, fine, mid, rows), state, cost=8000000)]
    ppermute x3, waiting for transfers between devices: 5.02 us -> 5.96 us  [exchange(): far = lax.ppermute(far, ('member', 'wide'), chip_swap)]
  transfers between devices with their start and end apart: 7 -> 7, of which waited for: 3 -> 3; matrix products, arithmetic and copies ran while one was open for 0% -> 0% of each run, Pallas kernels for 12% -> 10%
where the time goes in v4:
time: 37.5 us; the launch traced here: 37.3 us
  blocking collectives  13.3 us (35%)
  Pallas kernels  9.53 us (25%)
  starting transfers between devices  7.87 us (21%)
  waiting for transfers between devices  5.97 us (16%)
  between operations  0.69 us (2%)
    all_to_all x1, blocking collectives, shards(): same = lax.all_to_all(b3, 'wide', 0, 0, axis_index_groups=cores)  13.3 us
    ppermute x3, waiting for transfers between devices, exchange(): far = lax.ppermute(far, ('member', 'wide'), chip_swap)  5.96 us
    ppermute x3, starting transfers between devices, exchange(): far = lax.ppermute(far, ('member', 'wide'), chip_swap)  5.53 us
    pallas_call x1, Pallas kernels, shards(): call(functools.partial(rise_kernel, (fine, mid, two, three), rows), [shap...  2.37 us
    ppermute x3, starting transfers between devices, exchange(): near = lax.ppermute(near, 'wide', core_swap)  2.34 us
    pallas_call x1, Pallas kernels, shards(): call(functools.partial(coarse_kernel, (fine, three, four), rows), [shape(...  1.99 us
    pallas_call x1, Pallas kernels, shards(): call(functools.partial(inner_kernel, fine, mid, rows), state, cost=8000000)  1.56 us
    pallas_call x1, Pallas kernels, shards(): call(functools.partial(pack_kernel, fine, rows), [shape(4, total * fine.s...  1.32 us
  transfers between devices with their start and end apart: 7, of which 3 were waited for; matrix products, arithmetic and copies ran while one was open for 0% of the time, Pallas kernels for 10%

profile of v4, /device:TPU:0, one launch (start us, length us, event | category | flops | bytes accessed | tf_op | source)
XLA Modules:
  0.0 37.3 jit_solution(5633882541799136617)
XLA Ops:
  0.6 1.3 %shard_map.41 = (f32[4,704,128]{2,1,0:T(8,128)S(1)}, f32[4,96,128]{2,1,0:T(8,128)S(1)}, f32[4,96,128]{2,1,0:T(8,128)S(1)}) custom-call(f32[2,16,4096]{2,1,0:T(8,128)} %p_ref.1, f32[2,16,4096]{2,1,0:T(8,128)} %q_ref.1), custom_call_target="tpu_custom_call" | custom-call | tf_op jit(solution)/shard_map/pallas_call | solution.py:746
  2.0 0.6 %collective-permute-start = (f32[4,96,128]{2,1,0:T(8,128)S(1)}, f32[4,96,128]{2,1,0:T(8,128)S(1)}, u32[]{:S(2)}, u32[]{:S(2)}) collective-permute-start(f32[4,96,128]{2,1,0:T(8,128)S(1)} %get-tuple-element.33), channel_id=1, source_target_pairs={{0,1},{1,0},{2,3},{3,2},{4,5},{5,4},{6,7},{7,6},{8,9},{9,8},{10,11... | collective-permute-start | bytes 589832 | tf_op jit(solution)/shard_map/ppermute | solution.py:741
  2.5 2.6 %collective-permute-start.1 = (f32[4,96,128]{2,1,0:T(8,128)S(1)}, f32[4,96,128]{2,1,0:T(8,128)S(1)}, u32[]{:S(2)}, u32[]{:S(2)}) collective-permute-start(f32[4,96,128]{2,1,0:T(8,128)S(1)} %get-tuple-element.34), channel_id=1, source_target_pairs={{0,16},{15,31},{16,0},{31,15},{1,2},{2,1},{3,4},{4,3},{5,6},{6,5},... | collective-permute-start | bytes 589832 | tf_op jit(solution)/shard_map/ppermute | solution.py:740
  5.1 1.6 %shard_map.42 = (f32[4,704,128]{2,1,0:T(8,128)S(1)}, f32[4,704,128]{2,1,0:T(8,128)S(1)}, f32[2,704,128]{2,1,0:T(8,128)S(1)}, f32[2,704,128]{2,1,0:T(8,128)S(1)},...) custom-call(f32[4,704,128]{2,1,0:T(8,128)S(1)} %get-tuple-element.26.ext.refs_0_), custom_call_target="tpu_custom_call" | custom-call | flops 8000000 | bytes 1000000 | tf_op jit(solution)/shard_map/pallas_call | solution.py:761
  6.6 0.0 collective-permute-done.refs_7_
  6.6 2.1 %collective-permute-done.1.refs_8_ = f32[4,96,128]{2,1,0:T(8,128)S(1)} collective-permute-done((f32[4,96,128]{2,1,0:T(8,128)S(1)}, f32[4,96,128]{2,1,0:T(8,128)S(1)}, u32[]{:S(2)}, u32[]{:S(2)}) %collective-permute-start.1) | collective-permute-done | bytes 196640 | tf_op jit(solution)/shard_map/ppermute | solution.py:740
  8.7 1.2 %shard_map.43 = (f32[4,704,128]{2,1,0:T(8,128)S(1)}, f32[4,704,128]{2,1,0:T(8,128)S(1)}, f32[4,704,128]{2,1,0:T(8,128)S(1)}, f32[2,704,128]{2,1,0:T(8,128)S(1)},...) custom-call(f32[4,704,128]{2,1,0:T(8,128)S(1)} %get-tuple-element.26, ...), custom_call_target="tpu_custom_call", output_to_operand_aliasing={{0}: (0, {}), {1}: (1, {}), {2}: (2, {}), {3}: (3, {}), {4}... | custom-call | tf_op jit(solution)/shard_map/pallas_call | solution.py:767
  9.9 1.3 %collective-permute-start.2 = (f32[2,96,128]{2,1,0:T(8,128)S(1)}, f32[2,96,128]{2,1,0:T(8,128)S(1)}, u32[]{:S(2)}, u32[]{:S(2)}) collective-permute-start(f32[2,96,128]{2,1,0:T(8,128)S(1)} %get-tuple-element.36), channel_id=1, source_target_pairs={{0,1},{1,0},{2,3},{3,2},{4,5},{5,4},{6,7},{7,6},{8,9},{9,8},{10,11... | collective-permute-start | bytes 294920 | tf_op jit(solution)/shard_map/ppermute | solution.py:741
  11.2 1.5 %collective-permute-start.3 = (f32[2,96,128]{2,1,0:T(8,128)S(1)}, f32[2,96,128]{2,1,0:T(8,128)S(1)}, u32[]{:S(2)}, u32[]{:S(2)}) collective-permute-start(f32[2,96,128]{2,1,0:T(8,128)S(1)} %get-tuple-element.37), channel_id=1, source_target_pairs={{0,16},{15,31},{16,0},{31,15},{1,2},{2,1},{3,4},{4,3},{5,6},{6,5},... | collective-permute-start | bytes 294920 | tf_op jit(solution)/shard_map/ppermute | solution.py:740
  12.7 0.0 collective-permute-done.2.near_ref
  12.7 3.1 %collective-permute-done.3.far_ref = f32[2,96,128]{2,1,0:T(8,128)S(1)} collective-permute-done((f32[2,96,128]{2,1,0:T(8,128)S(1)}, f32[2,96,128]{2,1,0:T(8,128)S(1)}, u32[]{:S(2)}, u32[]{:S(2)}) %collective-permute-start.3) | collective-permute-done | bytes 98336 | tf_op jit(solution)/shard_map/ppermute | solution.py:740
  15.8 1.1 %shard_map.44 = (f32[2,320,128]{2,1,0:T(8,128)S(1)}, f32[2,320,128]{2,1,0:T(8,128)S(1)}, f32[2,96,128]{2,1,0:T(8,128)S(1)}, f32[2,96,128]{2,1,0:T(8,128)S(1)}, f...) custom-call(f32[2,128,128]{2,1,0:T(8,128)S(1)} %get-tuple-element.35.b_own, ...), custom_call_target="tpu_custom_call" | custom-call | tf_op jit(solution)/shard_map/pallas_call | solution.py:778
  16.9 13.3 %all_to_all.5.same_ref = f32[8,2,8,128]{3,2,1,0:T(8,128)S(1)} all-to-all(f32[8,2,8,128]{3,2,1,0:T(8,128)S(1)} %get-tuple-element.39), channel_id=1, replica_groups={{0,2,4,6,8,10,12,14},{1,3,5,7,9,11,13,15},{16,18,20,22,24,26,28,30},{17..., dimensions={0} | all-to-all | bytes 131072 | tf_op jit(solution)/shard_map/all_to_all | solution.py:796
  30.2 0.0 collective-permute-start.4
  30.2 0.5 %collective-permute-start.5 = (f32[2,64,128]{2,1,0:T(8,128)S(1)}, f32[2,64,128]{2,1,0:T(8,128)S(1)}, u32[]{:S(2)}, u32[]{:S(2)}) collective-permute-start(f32[2,64,128]{2,1,0:T(8,128)S(1)} %get-tuple-element.43), channel_id=1, source_target_pairs={{0,1},{1,0},{2,3},{3,2},{4,5},{5,4},{6,7},{7,6},{8,9},{9,8},{10,11... | collective-permute-start | bytes 196616 | tf_op jit(solution)/shard_map/ppermute | solution.py:741
  30.7 1.5 %collective-permute-start.6 = (f32[2,64,128]{2,1,0:T(8,128)S(1)}, f32[2,64,128]{2,1,0:T(8,128)S(1)}, u32[]{:S(2)}, u32[]{:S(2)}) collective-permute-start(f32[2,64,128]{2,1,0:T(8,128)S(1)} %get-tuple-element.44), channel_id=1, source_target_pairs={{0,16},{15,31},{16,0},{31,15},{1,2},{2,1},{3,4},{4,3},{5,6},{6,5},... | collective-permute-start | bytes 196616 | tf_op jit(solution)/shard_map/ppermute | solution.py:740
  32.2 0.0 collective-permute-done.4.other_ref
  32.2 2.0 %shard_map.45 = (f32[2,48,128]{2,1,0:T(8,128)S(1)}, f32[2,16,4096]{2,1,0:T(8,128)}) custom-call(f32[8,2,8,128]{3,2,1,0:T(8,128)S(1)} %all_to_all.5.same_ref, f32[8,2,8,128]{3,2,1,0:T(8,128)S(1)} %collective-permute-done.4.other_ref, f32[2,704,128]{2,1,0:T(8,128)S(1)} %get-tuple-element.40.b0_ref), custom_call_target="tpu_custom_call" | custom-call | flops 5000000 | bytes 625000 | tf_op jit(solution)/shard_map/pallas_call | solution.py:800
  34.2 0.0 collective-permute-done.5.near_ref
  34.2 0.8 %collective-permute-done.6.far_ref = f32[2,64,128]{2,1,0:T(8,128)S(1)} collective-permute-done((f32[2,64,128]{2,1,0:T(8,128)S(1)}, f32[2,64,128]{2,1,0:T(8,128)S(1)}, u32[]{:S(2)}, u32[]{:S(2)}) %collective-permute-start.6) | collective-permute-done | bytes 65568 | tf_op jit(solution)/shard_map/ppermute | solution.py:740
  35.0 2.4 %shard_map.46 = (f32[2,16,4096]{2,1,0:T(8,128)}, f32[2,704,128]{2,1,0:T(8,128)S(1)}) custom-call(f32[2,48,128]{2,1,0:T(8,128)S(1)} %get-tuple-element.42.v3_ref, f32[2,64,128]{2,1,0:T(8,128)S(1)} %collective-permute-done.5.near_ref, f32[2,64,128]{2,1,0:T(8,128)S(1)} %collective-permute-done.6.far_ref, ...), custom_call_target="tpu_custom_call", output_to_operand_aliasing={{1}: (8, {})} | custom-call | tf_op jit(solution)/shard_map/pallas_call | solution.py:809
Async XLA Ops:
  2.0 4.7 %collective-permute-start = (f32[4,96,128]{2,1,0:T(8,128)S(1)}, f32[4,96,128]{2,1,0:T(8,128)S(1)}, u32[]{:S(2)}, u32[]{:S(2)}) collective-permute-start(f32[4,96,128]{2,1,0:T(8,128)S(1)} %get-tuple-element.33), channel_id=1, source_target_pairs={{0,1},{1,0},{2,3},{3,2},{4,5},{5,4},{6,7},{7,6},{8,9},{9,8},{10,11... | collective-permute-start | bytes 589832 | tf_op jit(solution)/shard_map/ppermute | solution.py:741
  2.5 6.2 %collective-permute-start.1 = (f32[4,96,128]{2,1,0:T(8,128)S(1)}, f32[4,96,128]{2,1,0:T(8,128)S(1)}, u32[]{:S(2)}, u32[]{:S(2)}) collective-permute-start(f32[4,96,128]{2,1,0:T(8,128)S(1)} %get-tuple-element.34), channel_id=1, source_target_pairs={{0,16},{15,31},{16,0},{31,15},{1,2},{2,1},{3,4},{4,3},{5,6},{6,5},... | collective-permute-start | bytes 589832 | tf_op jit(solution)/shard_map/ppermute | solution.py:740
  9.9 2.8 %collective-permute-start.2 = (f32[2,96,128]{2,1,0:T(8,128)S(1)}, f32[2,96,128]{2,1,0:T(8,128)S(1)}, u32[]{:S(2)}, u32[]{:S(2)}) collective-permute-start(f32[2,96,128]{2,1,0:T(8,128)S(1)} %get-tuple-element.36), channel_id=1, source_target_pairs={{0,1},{1,0},{2,3},{3,2},{4,5},{5,4},{6,7},{7,6},{8,9},{9,8},{10,11... | collective-permute-start | bytes 294920 | tf_op jit(solution)/shard_map/ppermute | solution.py:741
  11.2 4.6 %collective-permute-start.3 = (f32[2,96,128]{2,1,0:T(8,128)S(1)}, f32[2,96,128]{2,1,0:T(8,128)S(1)}, u32[]{:S(2)}, u32[]{:S(2)}) collective-permute-start(f32[2,96,128]{2,1,0:T(8,128)S(1)} %get-tuple-element.37), channel_id=1, source_target_pairs={{0,16},{15,31},{16,0},{31,15},{1,2},{2,1},{3,4},{4,3},{5,6},{6,5},... | collective-permute-start | bytes 294920 | tf_op jit(solution)/shard_map/ppermute | solution.py:740
  30.2 2.0 %collective-permute-start.4 = (f32[8,2,8,128]{3,2,1,0:T(8,128)S(1)}, f32[8,2,8,128]{3,2,1,0:T(8,128)S(1)}, u32[]{:S(2)}, u32[]{:S(2)}) collective-permute-start(f32[8,2,8,128]{3,2,1,0:T(8,128)S(1)} %all_to_all.5.same_ref), channel_id=1, source_target_pairs={{0,1},{1,0},{2,3},{3,2},{4,5},{5,4},{6,7},{7,6},{8,9},{9,8},{10,11... | collective-permute-start | bytes 196616 | tf_op jit(solution)/shard_map/ppermute | solution.py:797
  30.2 4.0 %collective-permute-start.5 = (f32[2,64,128]{2,1,0:T(8,128)S(1)}, f32[2,64,128]{2,1,0:T(8,128)S(1)}, u32[]{:S(2)}, u32[]{:S(2)}) collective-permute-start(f32[2,64,128]{2,1,0:T(8,128)S(1)} %get-tuple-element.43), channel_id=1, source_target_pairs={{0,1},{1,0},{2,3},{3,2},{4,5},{5,4},{6,7},{7,6},{8,9},{9,8},{10,11... | collective-permute-start | bytes 196616 | tf_op jit(solution)/shard_map/ppermute | solution.py:741
  30.7 4.3 %collective-permute-start.6 = (f32[2,64,128]{2,1,0:T(8,128)S(1)}, f32[2,64,128]{2,1,0:T(8,128)S(1)}, u32[]{:S(2)}, u32[]{:S(2)}) collective-permute-start(f32[2,64,128]{2,1,0:T(8,128)S(1)} %get-tuple-element.44), channel_id=1, source_target_pairs={{0,16},{15,31},{16,0},{31,15},{1,2},{2,1},{3,4},{4,3},{5,6},{6,5},... | collective-permute-start | bytes 196616 | tf_op jit(solution)/shard_map/ppermute | solution.py:740

commit v5 on v4

--- a/solution.py
+++ b/solution.py
@@ -12,6 +12,7 @@
 SUBS = 8
 HALO = 3
 MID_HALO = 6
+LATE = 2
 TWO_HALO = 4
 RELAX = 0.8
 COUPLING = (0.02, 0.04)
@@ -361,13 +362,22 @@
     row_blocks(low, high, block, body)
 
 
-def inner_kernel(level, coarse, rows, ext, e_ref, w_ref, b_ref, v_one, v_two, bc_ref):
+def inner_kernel(
+    level, coarse, rows, ext, e_ref, w_ref, b_ref, v_one, v_two, bc_ref, early_near, early_far
+):
     low, high = HALO, HALO + rows
     shift_rows(level, ext, e_ref, w_ref, low, high, 4)
     advance_rows(level, b_ref, ext, e_ref, w_ref, low + 1, high - 1, 2)
     sweep(level, v_one, 0, ext, 0, b_ref, 0, low + 2, high - 2, 4, (e_ref, w_ref))
     sweep(level, v_two, 0, v_one, 0, b_ref, 0, low + 3, high - 3, 4)
-    restrict(level, bc_ref, 0, coarse, v_two, HALO, b_ref, HALO, 2, rows // 2 - 2, 2)
+    restrict(level, bc_ref, 0, coarse, v_two, HALO, b_ref, HALO, LATE, rows // 2 - LATE, 2)
+    size = (MID_HALO - LATE) * coarse.size
+    first, last = LATE * coarse.size, (rows // 2 - MID_HALO) * coarse.size
+    _, odd, _, _ = place()
+    near = pl.multiple_of(jnp.where(odd == 1, first, last), SUBS)
+    far = pl.multiple_of(jnp.where(odd == 1, last, first), SUBS)
+    early_near[...] = bc_ref[:, pl.ds(near, size), :]
+    early_far[...] = bc_ref[:, pl.ds(far, size), :]
 
 
 def outer_kernel(level, coarse, rows, *refs):
@@ -398,9 +408,9 @@
     sweep(level, v_two, 0, v_one, 0, b_ref, 0, high - 3, total - 2, 4)
     trim(v_two)
     half = rows // 2
-    restrict(level, bc_ref, 0, coarse, v_two, HALO, b_ref, HALO, 0, 2, 2)
-    restrict(level, bc_ref, 0, coarse, v_two, HALO, b_ref, HALO, half - 2, half, 2)
-    send_edges(coarse, MID_HALO, 0, half, bc_ref, bc_near_ref, bc_far_ref)
+    restrict(level, bc_ref, 0, coarse, v_two, HALO, b_ref, HALO, 0, LATE, 2)
+    restrict(level, bc_ref, 0, coarse, v_two, HALO, b_ref, HALO, half - LATE, half, 2)
+    send_edges(coarse, LATE, 0, half, bc_ref, bc_near_ref, bc_far_ref)
 
 
 def emit(level, rows, b_ref, next_ref, native, sems):
@@ -419,8 +429,13 @@
     return copies
 
 
+def emit_kernel(level, rows, b_ref, next_ref, native, sems):
+    for copy in emit(level, rows, b_ref, next_ref, native, sems):
+        copy.wait()
+
+
 def middle_kernel(
-    fine, level, two, three, rows, b_own, near_ref, far_ref, v0_ref,
+    fine, level, two, three, rows, b_own, early_near, early_far, near_ref, far_ref, v0_ref,
     b_ref, v_ref, b2_ref, v2_ref, out_ref, two_near_ref, two_far_ref,
     v_one, w_two, b3,
 ):
@@ -429,7 +444,9 @@
     own = rows // 2
     edge = MID_HALO * level.size
     b_ref[:, edge : edge + rows * level.size, :] = b_own[...]
-    receive_edges(level, MID_HALO, MID_HALO, rows, b_ref, near_ref, far_ref)
+    receive_edges(level, LATE, MID_HALO, rows, b_ref, near_ref, far_ref)
+    early = MID_HALO - LATE
+    receive_edges(level, early, early, rows + 2 * LATE, b_ref, early_near, early_far)
     start(level, v_one, 0, b_ref, 0, 0, total, 4)
 
     def trim(ref, of, halo, n):
@@ -537,12 +554,10 @@
 
 
 def coarse_kernel(
-    levels, rows, same_ref, other_ref, b0_ref, out_ref, next_ref,
-    b3, v3, w3, b4, v4, native, sems,
+    levels, rows, same_ref, other_ref, out_ref, b3, v3, w3, b4, v4,
 ):
     me, odd, is_first, is_last = place()
-    fine, three, four = levels
-    copies = emit(fine, rows, b0_ref, next_ref, native, sems)
+    three, four = levels
     own = rows // 4
     chips = same_ref.shape[0]
     n3, n4 = chips * own, chips * own // 2
@@ -592,9 +607,6 @@
     @pl.when(is_last)
     def _():
         clear(out_ref, three, half + 2, half + 4)
-
-    for copy in copies:
-        copy.wait()
 
 
 def rise_kernel(
@@ -758,12 +770,14 @@
         shape(2, total * fine.size, LANES),
         shape(2, half * mid.size, LANES),
     ]
-    inner = call(
+    early = shape(2, (MID_HALO - LATE) * mid.size, LANES)
+    *inner, near_early, far_early = call(
         functools.partial(inner_kernel, fine, mid, rows),
-        state,
+        state + [early, early],
         cost=8000000,
     )(ext)
-    edge = shape(2, MID_HALO * mid.size, LANES)
+    near_early, far_early = exchange(near_early, far_early)
+    edge = shape(2, LATE * mid.size, LANES)
     outer = call(
         functools.partial(outer_kernel, fine, mid, rows),
         [shape(4, total * fine.size, LANES)] + state + [edge, edge],
@@ -791,21 +805,26 @@
             scratch(2, quarter + 2 * TWO_HALO, two),
             scratch(2, eighth, three),
         ],
-    )(b1, near, far, v0)
+    )(b1, near_early, far_early, near, far, v0)
     cores = [[i for i in range(count) if i % 2 == c] for c in range(2)]
     same = lax.all_to_all(b3, "wide", 0, 0, axis_index_groups=cores)
     other = lax.ppermute(same, "wide", core_swap)
     near, far = exchange(near, far)
+    vorticity_next = call(
+        functools.partial(emit_kernel, fine, rows),
+        shape(2, rows, columns),
+        [pltpu.VMEM((2, rows, columns), jnp.float32), pltpu.SemaphoreType.DMA((2, groups))],
+        cost=4000000,
+        out_specs=HBM,
+    )(b0)
     n3, n4 = count * eighth, count * eighth // 2
-    v3, vorticity_next = call(
-        functools.partial(coarse_kernel, (fine, three, four), rows),
-        [shape(2, (eighth + 4) * three.size, LANES), shape(2, rows, columns)],
+    v3 = call(
+        functools.partial(coarse_kernel, (three, four), rows),
+        shape(2, (eighth + 4) * three.size, LANES),
         [scratch(2, n3 + 2 * PAD, three)] * 3
-        + [scratch(2, n4, four), scratch(2, n4 + 2 * PAD, four)]
-        + [pltpu.VMEM((2, rows, columns), jnp.float32), pltpu.SemaphoreType.DMA((2, groups))],
+        + [scratch(2, n4, four), scratch(2, n4 + 2 * PAD, four)],
         cost=5000000,
-        out_specs=[VMEM, HBM],
-    )(same, other, b0)
+    )(same, other)
     stream_next, _ = call(
         functools.partial(rise_kernel, (fine, mid, two, three), rows),
         [shape(2, rows, columns), shape(2, total * fine.size, LANES)],

time: 37.5 us -> 37.4 us (level)
  waiting for transfers between devices: 5.97 us -> 2.9 us
  starting transfers between devices: 7.87 us -> 9.57 us
  Pallas kernels: 9.53 us -> 10.2 us
  blocking collectives: 13.3 us -> 13.9 us
    ppermute x3 -> x4, waiting for transfers between devices: 5.96 us -> 2.88 us  [exchange(): far = lax.ppermute(far, ('member', 'wide'), chip_swap)]
    ppermute x3 -> x4, starting transfers between devices: 5.53 us -> 7.03 us  [exchange(): far = lax.ppermute(far, ('member', 'wide'), chip_swap)]
    pallas_call x2 -> x3, Pallas kernels: 3.55 us -> 4.21 us  [the longest x1 1.85 us: shards(): call(functools.partial(coarse_kernel, (three, four), rows), shape(2, (eig...]
    all_to_all x1, blocking collectives: 13.3 us -> 13.9 us  [shards(): same = lax.all_to_all(b3, 'wide', 0, 0, axis_index_groups=cores)]
    ppermute x3 -> x4, starting transfers between devices: 2.34 us -> 2.55 us  [exchange(): near = lax.ppermute(near, 'wide', core_swap)]
  transfers between devices with their start and end apart: 7 -> 9, of which waited for: 3 -> 2; matrix products, arithmetic and copies ran while one was open for 0% -> 0% of each run, Pallas kernels for 10% -> 15%
where the time goes in v5:
time: 37.4 us; the launch traced here: 37.2 us
  blocking collectives  13.9 us (37%)
  Pallas kernels  10.2 us (27%)
  starting transfers between devices  9.57 us (26%)
  waiting for transfers between devices  2.9 us (8%)
  between operations  0.7 us (2%)
    all_to_all x1, blocking collectives, shards(): same = lax.all_to_all(b3, 'wide', 0, 0, axis_index_groups=cores)  13.9 us
    ppermute x4, starting transfers between devices, exchange(): far = lax.ppermute(far, ('member', 'wide'), chip_swap)  7.03 us
    ppermute x4, waiting for transfers between devices, exchange(): far = lax.ppermute(far, ('member', 'wide'), chip_swap)  2.88 us
    ppermute x4, starting transfers between devices, exchange(): near = lax.ppermute(near, 'wide', core_swap)  2.55 us
    pallas_call x1, Pallas kernels, shards(): call(functools.partial(rise_kernel, (fine, mid, two, three), rows), [shap...  2.37 us
    pallas_call x1, Pallas kernels, shards(): call(functools.partial(coarse_kernel, (three, four), rows), shape(2, (eig...  1.85 us
    pallas_call x1, Pallas kernels, shards(): call(functools.partial(inner_kernel, fine, mid, rows), state + [early, ea...  1.5 us
    pallas_call x1, Pallas kernels, shards(): call(functools.partial(pack_kernel, fine, rows), [shape(4, total * fine.s...  1.32 us
  transfers between devices with their start and end apart: 9, of which 2 were waited for; matrix products, arithmetic and copies ran while one was open for 0% of the time, Pallas kernels for 15%

profile of v5, /device:TPU:0, one launch (start us, length us, event | category | flops | bytes accessed | tf_op | source)
XLA Modules:
  0.0 37.2 jit_solution(3425750624350299734)
XLA Ops:
  0.6 1.3 %shard_map.41 = (f32[4,704,128]{2,1,0:T(8,128)S(1)}, f32[4,96,128]{2,1,0:T(8,128)S(1)}, f32[4,96,128]{2,1,0:T(8,128)S(1)}) custom-call(f32[2,16,4096]{2,1,0:T(8,128)} %p_ref.1, f32[2,16,4096]{2,1,0:T(8,128)} %q_ref.1), custom_call_target="tpu_custom_call" | custom-call | tf_op jit(solution)/shard_map/pallas_call | solution.py:758
  2.0 0.6 %collective-permute-start = (f32[4,96,128]{2,1,0:T(8,128)S(1)}, f32[4,96,128]{2,1,0:T(8,128)S(1)}, u32[]{:S(2)}, u32[]{:S(2)}) collective-permute-start(f32[4,96,128]{2,1,0:T(8,128)S(1)} %get-tuple-element.33), channel_id=1, source_target_pairs={{0,1},{1,0},{2,3},{3,2},{4,5},{5,4},{6,7},{7,6},{8,9},{9,8},{10,11... | collective-permute-start | bytes 589832 | tf_op jit(solution)/shard_map/ppermute | solution.py:753
  2.5 2.6 %collective-permute-start.1 = (f32[4,96,128]{2,1,0:T(8,128)S(1)}, f32[4,96,128]{2,1,0:T(8,128)S(1)}, u32[]{:S(2)}, u32[]{:S(2)}) collective-permute-start(f32[4,96,128]{2,1,0:T(8,128)S(1)} %get-tuple-element.34), channel_id=1, source_target_pairs={{0,16},{15,31},{16,0},{31,15},{1,2},{2,1},{3,4},{4,3},{5,6},{6,5},... | collective-permute-start | bytes 589832 | tf_op jit(solution)/shard_map/ppermute | solution.py:752
  5.1 1.5 %shard_map.42 = (f32[4,704,128]{2,1,0:T(8,128)S(1)}, f32[4,704,128]{2,1,0:T(8,128)S(1)}, f32[2,704,128]{2,1,0:T(8,128)S(1)}, f32[2,704,128]{2,1,0:T(8,128)S(1)},...) custom-call(f32[4,704,128]{2,1,0:T(8,128)S(1)} %get-tuple-element.26, ...), custom_call_target="tpu_custom_call" | custom-call | flops 8000000 | bytes 1000000 | tf_op jit(solution)/shard_map/pallas_call | solution.py:774
  6.6 0.2 collective-permute-start.2
  6.8 1.5 %collective-permute-start.3 = (f32[2,64,128]{2,1,0:T(8,128)S(1)}, f32[2,64,128]{2,1,0:T(8,128)S(1)}, u32[]{:S(2)}, u32[]{:S(2)}) collective-permute-start(f32[2,64,128]{2,1,0:T(8,128)S(1)} %get-tuple-element.38), channel_id=1, source_target_pairs={{0,16},{15,31},{16,0},{31,15},{1,2},{2,1},{3,4},{4,3},{5,6},{6,5},... | collective-permute-start | bytes 196616 | tf_op jit(solution)/shard_map/ppermute | solution.py:752
  8.3 0.0 collective-permute-done.refs_7_
  8.3 0.4 %collective-permute-done.1.refs_8_ = f32[4,96,128]{2,1,0:T(8,128)S(1)} collective-permute-done((f32[4,96,128]{2,1,0:T(8,128)S(1)}, f32[4,96,128]{2,1,0:T(8,128)S(1)}, u32[]{:S(2)}, u32[]{:S(2)}) %collective-permute-start.1) | collective-permute-done | bytes 196640 | tf_op jit(solution)/shard_map/ppermute | solution.py:752
  8.7 1.2 %shard_map.43 = (f32[4,704,128]{2,1,0:T(8,128)S(1)}, f32[4,704,128]{2,1,0:T(8,128)S(1)}, f32[4,704,128]{2,1,0:T(8,128)S(1)}, f32[2,704,128]{2,1,0:T(8,128)S(1)},...) custom-call(f32[4,704,128]{2,1,0:T(8,128)S(1)} %get-tuple-element.26, ...), custom_call_target="tpu_custom_call", output_to_operand_aliasing={{0}: (0, {}), {1}: (1, {}), {2}: (2, {}), {3}: (3, {}), {4}... | custom-call | tf_op jit(solution)/shard_map/pallas_call | solution.py:781
  9.9 1.3 %collective-permute-start.4 = (f32[2,32,128]{2,1,0:T(8,128)S(1)}, f32[2,32,128]{2,1,0:T(8,128)S(1)}, u32[]{:S(2)}, u32[]{:S(2)}) collective-permute-start(f32[2,32,128]{2,1,0:T(8,128)S(1)} %get-tuple-element.39), channel_id=1, source_target_pairs={{0,1},{1,0},{2,3},{3,2},{4,5},{5,4},{6,7},{7,6},{8,9},{9,8},{10,11... | collective-permute-start | bytes 98312 | tf_op jit(solution)/shard_map/ppermute | solution.py:753
  11.2 1.5 %collective-permute-start.5 = (f32[2,32,128]{2,1,0:T(8,128)S(1)}, f32[2,32,128]{2,1,0:T(8,128)S(1)}, u32[]{:S(2)}, u32[]{:S(2)}) collective-permute-start(f32[2,32,128]{2,1,0:T(8,128)S(1)} %get-tuple-element.40), channel_id=1, source_target_pairs={{0,16},{15,31},{16,0},{31,15},{1,2},{2,1},{3,4},{4,3},{5,6},{6,5},... | collective-permute-start | bytes 98312 | tf_op jit(solution)/shard_map/ppermute | solution.py:752
  12.7 0.0 collective-permute-done.2.early_near
  12.7 0.0 collective-permute-done.3.early_far
  12.7 2.4 %collective-permute-done.5.far_ref = f32[2,32,128]{2,1,0:T(8,128)S(1)} collective-permute-done((f32[2,32,128]{2,1,0:T(8,128)S(1)}, f32[2,32,128]{2,1,0:T(8,128)S(1)}, u32[]{:S(2)}, u32[]{:S(2)}) %collective-permute-start.5) | collective-permute-done | bytes 32800 | tf_op jit(solution)/shard_map/ppermute | solution.py:752
  15.1 1.1 %shard_map.45 = (f32[2,320,128]{2,1,0:T(8,128)S(1)}, f32[2,320,128]{2,1,0:T(8,128)S(1)}, f32[2,96,128]{2,1,0:T(8,128)S(1)}, f32[2,96,128]{2,1,0:T(8,128)S(1)}, f...) custom-call(f32[2,128,128]{2,1,0:T(8,128)S(1)} %get-tuple-element.36.b_own, ...), custom_call_target="tpu_custom_call" | custom-call | tf_op jit(solution)/shard_map/pallas_call | solution.py:792
  16.2 13.9 %all_to_all.5.same_ref = f32[8,2,8,128]{3,2,1,0:T(8,128)S(1)} all-to-all(f32[8,2,8,128]{3,2,1,0:T(8,128)S(1)} %get-tuple-element.42), channel_id=1, replica_groups={{0,2,4,6,8,10,12,14},{1,3,5,7,9,11,13,15},{16,18,20,22,24,26,28,30},{17..., dimensions={0} | all-to-all | bytes 131072 | tf_op jit(solution)/shard_map/all_to_all | solution.py:810
  30.1 0.0 collective-permute-start.6
  30.1 0.5 %collective-permute-start.7 = (f32[2,64,128]{2,1,0:T(8,128)S(1)}, f32[2,64,128]{2,1,0:T(8,128)S(1)}, u32[]{:S(2)}, u32[]{:S(2)}) collective-permute-start(f32[2,64,128]{2,1,0:T(8,128)S(1)} %get-tuple-element.43), channel_id=1, source_target_pairs={{0,1},{1,0},{2,3},{3,2},{4,5},{5,4},{6,7},{7,6},{8,9},{9,8},{10,11... | collective-permute-start | bytes 196616 | tf_op jit(solution)/shard_map/ppermute | solution.py:753
  30.6 1.5 %collective-permute-start.8 = (f32[2,64,128]{2,1,0:T(8,128)S(1)}, f32[2,64,128]{2,1,0:T(8,128)S(1)}, u32[]{:S(2)}, u32[]{:S(2)}) collective-permute-start(f32[2,64,128]{2,1,0:T(8,128)S(1)} %get-tuple-element.44), channel_id=1, source_target_pairs={{0,16},{15,31},{16,0},{31,15},{1,2},{2,1},{3,4},{4,3},{5,6},{6,5},... | collective-permute-start | bytes 196616 | tf_op jit(solution)/shard_map/ppermute | solution.py:752
  32.1 0.9 %shard_map.44 = f32[2,16,4096]{2,1,0:T(8,128)} custom-call(f32[2,704,128]{2,1,0:T(8,128)S(1)} %get-tuple-element.35.b_ref.b0_ref), custom_call_target="tpu_custom_call" | custom-call | flops 4000000 | bytes 500000 | tf_op jit(solution)/shard_map/pallas_call | solution.py:813
  32.9 0.0 collective-permute-done.6.other_ref
  32.9 1.9 %shard_map.46.v3_ref = f32[2,48,128]{2,1,0:T(8,128)S(1)} custom-call(f32[8,2,8,128]{3,2,1,0:T(8,128)S(1)} %all_to_all.5.same_ref, f32[8,2,8,128]{3,2,1,0:T(8,128)S(1)} %collective-permute-done.6.other_ref), custom_call_target="tpu_custom_call" | custom-call | flops 5000000 | bytes 625000 | tf_op jit(solution)/shard_map/pallas_call | solution.py:821
  34.8 0.0 collective-permute-done.8.far_ref
  34.9 2.4 %shard_map.47 = (f32[2,16,4096]{2,1,0:T(8,128)}, f32[2,704,128]{2,1,0:T(8,128)S(1)}) custom-call(f32[2,48,128]{2,1,0:T(8,128)S(1)} %shard_map.46.v3_ref, f32[2,64,128]{2,1,0:T(8,128)S(1)} %collective-permute-done.7.near_ref, f32[2,64,128]{2,1,0:T(8,128)S(1)} %collective-permute-done.8.far_ref, ...), custom_call_target="tpu_custom_call", output_to_operand_aliasing={{1}: (8, {})} | custom-call | tf_op jit(solution)/shard_map/pallas_call | solution.py:828
  (2 shorter events, 0.0 us)
Async XLA Ops:
  2.0 6.3 %collective-permute-start = (f32[4,96,128]{2,1,0:T(8,128)S(1)}, f32[4,96,128]{2,1,0:T(8,128)S(1)}, u32[]{:S(2)}, u32[]{:S(2)}) collective-permute-start(f32[4,96,128]{2,1,0:T(8,128)S(1)} %get-tuple-element.33), channel_id=1, source_target_pairs={{0,1},{1,0},{2,3},{3,2},{4,5},{5,4},{6,7},{7,6},{8,9},{9,8},{10,11... | collective-permute-start | bytes 589832 | tf_op jit(solution)/shard_map/ppermute | solution.py:753
  2.5 6.2 %collective-permute-start.1 = (f32[4,96,128]{2,1,0:T(8,128)S(1)}, f32[4,96,128]{2,1,0:T(8,128)S(1)}, u32[]{:S(2)}, u32[]{:S(2)}) collective-permute-start(f32[4,96,128]{2,1,0:T(8,128)S(1)} %get-tuple-element.34), channel_id=1, source_target_pairs={{0,16},{15,31},{16,0},{31,15},{1,2},{2,1},{3,4},{4,3},{5,6},{6,5},... | collective-permute-start | bytes 589832 | tf_op jit(solution)/shard_map/ppermute | solution.py:752
  6.6 6.1 %collective-permute-start.2 = (f32[2,64,128]{2,1,0:T(8,128)S(1)}, f32[2,64,128]{2,1,0:T(8,128)S(1)}, u32[]{:S(2)}, u32[]{:S(2)}) collective-permute-start(f32[2,64,128]{2,1,0:T(8,128)S(1)} %get-tuple-element.37), channel_id=1, source_target_pairs={{0,1},{1,0},{2,3},{3,2},{4,5},{5,4},{6,7},{7,6},{8,9},{9,8},{10,11... | collective-permute-start | bytes 196616 | tf_op jit(solution)/shard_map/ppermute | solution.py:753
  6.8 5.9 %collective-permute-start.3 = (f32[2,64,128]{2,1,0:T(8,128)S(1)}, f32[2,64,128]{2,1,0:T(8,128)S(1)}, u32[]{:S(2)}, u32[]{:S(2)}) collective-permute-start(f32[2,64,128]{2,1,0:T(8,128)S(1)} %get-tuple-element.38), channel_id=1, source_target_pairs={{0,16},{15,31},{16,0},{31,15},{1,2},{2,1},{3,4},{4,3},{5,6},{6,5},... | collective-permute-start | bytes 196616 | tf_op jit(solution)/shard_map/ppermute | solution.py:752
  9.9 2.8 %collective-permute-start.4 = (f32[2,32,128]{2,1,0:T(8,128)S(1)}, f32[2,32,128]{2,1,0:T(8,128)S(1)}, u32[]{:S(2)}, u32[]{:S(2)}) collective-permute-start(f32[2,32,128]{2,1,0:T(8,128)S(1)} %get-tuple-element.39), channel_id=1, source_target_pairs={{0,1},{1,0},{2,3},{3,2},{4,5},{5,4},{6,7},{7,6},{8,9},{9,8},{10,11... | collective-permute-start | bytes 98312 | tf_op jit(solution)/shard_map/ppermute | solution.py:753
  11.2 3.9 %collective-permute-start.5 = (f32[2,32,128]{2,1,0:T(8,128)S(1)}, f32[2,32,128]{2,1,0:T(8,128)S(1)}, u32[]{:S(2)}, u32[]{:S(2)}) collective-permute-start(f32[2,32,128]{2,1,0:T(8,128)S(1)} %get-tuple-element.40), channel_id=1, source_target_pairs={{0,16},{15,31},{16,0},{31,15},{1,2},{2,1},{3,4},{4,3},{5,6},{6,5},... | collective-permute-start | bytes 98312 | tf_op jit(solution)/shard_map/ppermute | solution.py:752
  30.1 2.9 %collective-permute-start.6 = (f32[8,2,8,128]{3,2,1,0:T(8,128)S(1)}, f32[8,2,8,128]{3,2,1,0:T(8,128)S(1)}, u32[]{:S(2)}, u32[]{:S(2)}) collective-permute-start(f32[8,2,8,128]{3,2,1,0:T(8,128)S(1)} %all_to_all.5.same_ref), channel_id=1, source_target_pairs={{0,1},{1,0},{2,3},{3,2},{4,5},{5,4},{6,7},{7,6},{8,9},{9,8},{10,11... | collective-permute-start | bytes 196616 | tf_op jit(solution)/shard_map/ppermute | solution.py:811
  30.1 4.7 %collective-permute-start.7 = (f32[2,64,128]{2,1,0:T(8,128)S(1)}, f32[2,64,128]{2,1,0:T(8,128)S(1)}, u32[]{:S(2)}, u32[]{:S(2)}) collective-permute-start(f32[2,64,128]{2,1,0:T(8,128)S(1)} %get-tuple-element.43), channel_id=1, source_target_pairs={{0,1},{1,0},{2,3},{3,2},{4,5},{5,4},{6,7},{7,6},{8,9},{9,8},{10,11... | collective-permute-start | bytes 196616 | tf_op jit(solution)/shard_map/ppermute | solution.py:753
  30.6 4.3 %collective-permute-start.8 = (f32[2,64,128]{2,1,0:T(8,128)S(1)}, f32[2,64,128]{2,1,0:T(8,128)S(1)}, u32[]{:S(2)}, u32[]{:S(2)}) collective-permute-start(f32[2,64,128]{2,1,0:T(8,128)S(1)} %get-tuple-element.44), channel_id=1, source_target_pairs={{0,16},{15,31},{16,0},{31,15},{1,2},{2,1},{3,4},{4,3},{5,6},{6,5},... | collective-permute-start | bytes 196616 | tf_op jit(solution)/shard_map/ppermute | solution.py:752

commit v6 on v5

--- a/solution.py
+++ b/solution.py
@@ -380,37 +380,41 @@
     early_far[...] = bc_ref[:, pl.ds(far, size), :]
 
 
-def outer_kernel(level, coarse, rows, *refs):
-    near_ref, far_ref = refs[7:9]
-    ext, e_ref, w_ref, b_ref, v_one, v_two, bc_ref, bc_near_ref, bc_far_ref = refs[9:]
-    _, _, is_first, is_last = place()
-    low, high = HALO, HALO + rows
+def outer_kernel(level, coarse, rows, far, *refs):
+    halo_ref = refs[7]
+    ext, e_ref, w_ref, b_ref, v_one, v_two, bc_ref, send_ref = refs[8:]
+    _, odd, is_first, is_last = place()
+    high, half = HALO + rows, rows // 2
     total = rows + 2 * HALO
-    receive_edges(level, HALO, HALO, rows, ext, near_ref, far_ref)
-    shift_rows(level, ext, e_ref, w_ref, 0, low, 3)
-    shift_rows(level, ext, e_ref, w_ref, high, total, 3)
-    advance_rows(level, b_ref, ext, e_ref, w_ref, 1, low + 1, 3)
-    advance_rows(level, b_ref, ext, e_ref, w_ref, high - 1, total - 1, 3)
-    sweep(level, v_one, 0, ext, 0, b_ref, 0, 1, low + 2, 4, (e_ref, w_ref))
-    sweep(level, v_one, 0, ext, 0, b_ref, 0, high - 2, total - 1, 4, (e_ref, w_ref))
+    top = odd == 0 if far else odd == 1
+
+    def pick(above, below):
+        return jnp.where(top, above, below)
+
+    outside = jnp.logical_and(far, jnp.logical_or(is_first, is_last))
+    size = HALO * level.size
+    edge = pl.ds(pl.multiple_of(pick(0, high) * level.size, SUBS), size)
+    halo = halo_ref[...]
+    ext[:, edge, :] = jnp.where(outside, 0.0, halo) if far else halo
+    shift_rows(level, ext, e_ref, w_ref, pick(0, high), HALO, HALO)
+    advance_rows(level, b_ref, ext, e_ref, w_ref, pick(1, high - 1), HALO, HALO)
+    count = HALO + 1
+    sides = (e_ref, w_ref)
+    sweep(level, v_one, 0, ext, 0, b_ref, 0, pick(1, high - 2), count, count, sides)
 
     def trim(ref):
-        @pl.when(is_first)
-        def _():
-            clear(ref, level, 0, HALO)
-
-        @pl.when(is_last)
-        def _():
-            clear(ref, level, high, total)
+        if far:
+            @pl.when(outside)
+            def _():
+                ref[:, edge, :] = jnp.zeros((2, size, LANES), jnp.float32)
 
     trim(v_one)
-    sweep(level, v_two, 0, v_one, 0, b_ref, 0, 2, low + 3, 4)
-    sweep(level, v_two, 0, v_one, 0, b_ref, 0, high - 3, total - 2, 4)
+    sweep(level, v_two, 0, v_one, 0, b_ref, 0, pick(2, total - 2 - count), count, count)
     trim(v_two)
-    half = rows // 2
-    restrict(level, bc_ref, 0, coarse, v_two, HALO, b_ref, HALO, 0, LATE, 2)
-    restrict(level, bc_ref, 0, coarse, v_two, HALO, b_ref, HALO, half - LATE, half, 2)
-    send_edges(coarse, LATE, 0, half, bc_ref, bc_near_ref, bc_far_ref)
+    late = pick(0, half - LATE)
+    restrict(level, bc_ref, 0, coarse, v_two, HALO, b_ref, HALO, late, LATE, LATE)
+    rows_of = pl.ds(pl.multiple_of(late * coarse.size, SUBS), LATE * coarse.size)
+    send_ref[...] = bc_ref[:, rows_of, :]
 
 
 def emit(level, rows, b_ref, next_ref, native, sems):
@@ -778,12 +782,18 @@
     )(ext)
     near_early, far_early = exchange(near_early, far_early)
     edge = shape(2, LATE * mid.size, LANES)
-    outer = call(
-        functools.partial(outer_kernel, fine, mid, rows),
-        [shape(4, total * fine.size, LANES)] + state + [edge, edge],
-        input_output_aliases={i: i for i in range(7)},
-    )(ext, *inner, near, far)
-    b0, v0, b1, near, far = outer[3], outer[5], outer[6], outer[7], outer[8]
+
+    def outer(far, arrays, halo):
+        return call(
+            functools.partial(outer_kernel, fine, mid, rows, far),
+            [shape(4, total * fine.size, LANES)] + state + [edge],
+            cost=4000000,
+            input_output_aliases={i: i for i in range(7)},
+        )(*arrays, halo)
+
+    *arrays, near = outer(False, [ext, *inner], near)
+    *arrays, far = outer(True, arrays, far)
+    b0, v0, b1 = arrays[3], arrays[5], arrays[6]
     near, far = exchange(near, far)
     chips = count // 2
     eighth = rows // 8

time: 37.4 us -> 35.4 us (0.947)
  waiting for transfers between devices: 2.9 us -> 0.9 us
  blocking collectives: 13.9 us -> 12.9 us
  starting transfers between devices: 9.57 us -> 10.2 us
    ppermute x4, waiting for transfers between devices: 2.88 us -> 0.61 us  [exchange(): far = lax.ppermute(far, ('member', 'wide'), chip_swap)]
    all_to_all x1, blocking collectives: 13.9 us -> 12.9 us  [shards(): same = lax.all_to_all(b3, 'wide', 0, 0, axis_index_groups=cores)]
    ppermute x4, starting transfers between devices: 2.55 us -> 2.94 us  [exchange(): near = lax.ppermute(near, 'wide', core_swap)]
    pallas_call x1 -> x2, Pallas kernels: 1.21 us -> 1.57 us  [outer(): call(functools.partial(outer_kernel, fine, mid, rows, far), [shape(4, tot...]
  transfers between devices with their start and end apart: 9 -> 9, of which waited for: 2 -> 2; matrix products, arithmetic and copies ran while one was open for 0% -> 0% of each run, Pallas kernels for 15% -> 16%
where the time goes in v6:
time: 35.4 us; the launch traced here: 35.2 us
  blocking collectives  12.9 us (36%)
  Pallas kernels  10.5 us (30%)
  starting transfers between devices  10.2 us (29%)
  waiting for transfers between devices  0.9 us (3%)
  between operations  0.72 us (2%)
    all_to_all x1, blocking collectives, shards(): same = lax.all_to_all(b3, 'wide', 0, 0, axis_index_groups=cores)  12.9 us
    ppermute x4, starting transfers between devices, exchange(): far = lax.ppermute(far, ('member', 'wide'), chip_swap)  7.27 us
    ppermute x4, starting transfers between devices, exchange(): near = lax.ppermute(near, 'wide', core_swap)  2.94 us
    pallas_call x1, Pallas kernels, shards(): call(functools.partial(rise_kernel, (fine, mid, two, three), rows), [shap...  2.37 us
    pallas_call x1, Pallas kernels, shards(): call(functools.partial(coarse_kernel, (three, four), rows), shape(2, (eig...  1.85 us
    pallas_call x2, Pallas kernels, outer(): call(functools.partial(outer_kernel, fine, mid, rows, far), [shape(4, tot...  1.57 us
    pallas_call x1, Pallas kernels, shards(): call(functools.partial(inner_kernel, fine, mid, rows), state + [early, ea...  1.5 us
    pallas_call x1, Pallas kernels, shards(): call(functools.partial(pack_kernel, fine, rows), [shape(4, total * fine.s...  1.32 us
  transfers between devices with their start and end apart: 9, of which 2 were waited for; matrix products, arithmetic and copies ran while one was open for 0% of the time, Pallas kernels for 16%

profile of v6, /device:TPU:0, one launch (start us, length us, event | category | flops | bytes accessed | tf_op | source)
XLA Modules:
  0.0 35.2 jit_solution(8131727918088480266)
XLA Ops:
  0.6 1.3 %shard_map.41 = (f32[4,704,128]{2,1,0:T(8,128)S(1)}, f32[4,96,128]{2,1,0:T(8,128)S(1)}, f32[4,96,128]{2,1,0:T(8,128)S(1)}) custom-call(f32[2,16,4096]{2,1,0:T(8,128)} %p_ref.1, f32[2,16,4096]{2,1,0:T(8,128)} %q_ref.1), custom_call_target="tpu_custom_call" | custom-call | tf_op jit(solution)/shard_map/pallas_call | solution.py:762
  2.0 0.6 %collective-permute-start = (f32[4,96,128]{2,1,0:T(8,128)S(1)}, f32[4,96,128]{2,1,0:T(8,128)S(1)}, u32[]{:S(2)}, u32[]{:S(2)}) collective-permute-start(f32[4,96,128]{2,1,0:T(8,128)S(1)} %get-tuple-element.40), channel_id=1, source_target_pairs={{0,1},{1,0},{2,3},{3,2},{4,5},{5,4},{6,7},{7,6},{8,9},{9,8},{10,11... | collective-permute-start | bytes 589832 | tf_op jit(solution)/shard_map/ppermute | solution.py:757
  2.5 2.6 %collective-permute-start.1 = (f32[4,96,128]{2,1,0:T(8,128)S(1)}, f32[4,96,128]{2,1,0:T(8,128)S(1)}, u32[]{:S(2)}, u32[]{:S(2)}) collective-permute-start(f32[4,96,128]{2,1,0:T(8,128)S(1)} %get-tuple-element.48), channel_id=1, source_target_pairs={{0,16},{15,31},{16,0},{31,15},{1,2},{2,1},{3,4},{4,3},{5,6},{6,5},... | collective-permute-start | bytes 589832 | tf_op jit(solution)/shard_map/ppermute | solution.py:756
  5.1 1.5 %shard_map.42 = (f32[4,704,128]{2,1,0:T(8,128)S(1)}, f32[4,704,128]{2,1,0:T(8,128)S(1)}, f32[2,704,128]{2,1,0:T(8,128)S(1)}, f32[2,704,128]{2,1,0:T(8,128)S(1)},...) custom-call(f32[4,704,128]{2,1,0:T(8,128)S(1)} %get-tuple-element.33, ...), custom_call_target="tpu_custom_call" | custom-call | flops 8000000 | bytes 1000000 | tf_op jit(solution)/shard_map/pallas_call | solution.py:778
  6.6 0.2 collective-permute-start.2
  6.8 1.5 %collective-permute-start.3 = (f32[2,64,128]{2,1,0:T(8,128)S(1)}, f32[2,64,128]{2,1,0:T(8,128)S(1)}, u32[]{:S(2)}, u32[]{:S(2)}) collective-permute-start(f32[2,64,128]{2,1,0:T(8,128)S(1)} %get-tuple-element.52), channel_id=1, source_target_pairs={{0,16},{15,31},{16,0},{31,15},{1,2},{2,1},{3,4},{4,3},{5,6},{6,5},... | collective-permute-start | bytes 196616 | tf_op jit(solution)/shard_map/ppermute | solution.py:756
  8.3 0.0 collective-permute-done.refs_7_
  8.3 0.8 %shard_map.43 = (f32[4,704,128]{2,1,0:T(8,128)S(1)}, f32[4,704,128]{2,1,0:T(8,128)S(1)}, f32[4,704,128]{2,1,0:T(8,128)S(1)}, f32[2,704,128]{2,1,0:T(8,128)S(1)},...) custom-call(f32[4,704,128]{2,1,0:T(8,128)S(1)} %get-tuple-element.33, ...), custom_call_target="tpu_custom_call", output_to_operand_aliasing={{0}: (0, {}), {1}: (1, {}), {2}: (2, {}), {3}: (3, {}), {4}... | custom-call | flops 4000000 | bytes 500000 | tf_op jit(solution)/shard_map/pallas_call | solution.py:787
  9.0 0.8 %shard_map.44 = (f32[4,704,128]{2,1,0:T(8,128)S(1)}, f32[4,704,128]{2,1,0:T(8,128)S(1)}, f32[4,704,128]{2,1,0:T(8,128)S(1)}, f32[2,704,128]{2,1,0:T(8,128)S(1)},...) custom-call(f32[4,704,128]{2,1,0:T(8,128)S(1)} %get-tuple-element.41, ...), custom_call_target="tpu_custom_call", output_to_operand_aliasing={{0}: (0, {}), {1}: (1, {}), {2}: (2, {}), {3}: (3, {}), {4}... | custom-call | flops 4000000 | bytes 500000 | tf_op jit(solution)/shard_map/pallas_call | solution.py:787
  9.9 1.7 %collective-permute-start.5 = (f32[2,32,128]{2,1,0:T(8,128)S(1)}, f32[2,32,128]{2,1,0:T(8,128)S(1)}, u32[]{:S(2)}, u32[]{:S(2)}) collective-permute-start(f32[2,32,128]{2,1,0:T(8,128)S(1)} %get-tuple-element.54), channel_id=1, source_target_pairs={{0,16},{15,31},{16,0},{31,15},{1,2},{2,1},{3,4},{4,3},{5,6},{6,5},... | collective-permute-start | bytes 98312 | tf_op jit(solution)/shard_map/ppermute | solution.py:756
  11.6 1.7 %collective-permute-start.4 = (f32[2,32,128]{2,1,0:T(8,128)S(1)}, f32[2,32,128]{2,1,0:T(8,128)S(1)}, u32[]{:S(2)}, u32[]{:S(2)}) collective-permute-start(f32[2,32,128]{2,1,0:T(8,128)S(1)} %get-tuple-element.53), channel_id=1, source_target_pairs={{0,1},{1,0},{2,3},{3,2},{4,5},{5,4},{6,7},{7,6},{8,9},{9,8},{10,11... | collective-permute-start | bytes 98312 | tf_op jit(solution)/shard_map/ppermute | solution.py:757
  13.3 0.0 collective-permute-done.2.early_near
  13.3 0.0 collective-permute-done.3.early_far
  13.3 0.6 %collective-permute-done.5.far_ref = f32[2,32,128]{2,1,0:T(8,128)S(1)} collective-permute-done((f32[2,32,128]{2,1,0:T(8,128)S(1)}, f32[2,32,128]{2,1,0:T(8,128)S(1)}, u32[]{:S(2)}, u32[]{:S(2)}) %collective-permute-start.5) | collective-permute-done | bytes 32800 | tf_op jit(solution)/shard_map/ppermute | solution.py:756
  13.9 0.3 collective-permute-done.4.near_ref
  14.1 1.1 %shard_map.46 = (f32[2,320,128]{2,1,0:T(8,128)S(1)}, f32[2,320,128]{2,1,0:T(8,128)S(1)}, f32[2,96,128]{2,1,0:T(8,128)S(1)}, f32[2,96,128]{2,1,0:T(8,128)S(1)}, f...) custom-call(f32[2,128,128]{2,1,0:T(8,128)S(1)} %get-tuple-element.50.b_own, ...), custom_call_target="tpu_custom_call" | custom-call | tf_op jit(solution)/shard_map/pallas_call | solution.py:802
  15.2 12.9 %all_to_all.5.same_ref = f32[8,2,8,128]{3,2,1,0:T(8,128)S(1)} all-to-all(f32[8,2,8,128]{3,2,1,0:T(8,128)S(1)} %get-tuple-element.56), channel_id=1, replica_groups={{0,2,4,6,8,10,12,14},{1,3,5,7,9,11,13,15},{16,18,20,22,24,26,28,30},{17..., dimensions={0} | all-to-all | bytes 131072 | tf_op jit(solution)/shard_map/all_to_all | solution.py:820
  28.1 0.0 collective-permute-start.6
  28.1 0.5 %collective-permute-start.7 = (f32[2,64,128]{2,1,0:T(8,128)S(1)}, f32[2,64,128]{2,1,0:T(8,128)S(1)}, u32[]{:S(2)}, u32[]{:S(2)}) collective-permute-start(f32[2,64,128]{2,1,0:T(8,128)S(1)} %get-tuple-element.57), channel_id=1, source_target_pairs={{0,1},{1,0},{2,3},{3,2},{4,5},{5,4},{6,7},{7,6},{8,9},{9,8},{10,11... | collective-permute-start | bytes 196616 | tf_op jit(solution)/shard_map/ppermute | solution.py:757
  28.6 1.5 %collective-permute-start.8 = (f32[2,64,128]{2,1,0:T(8,128)S(1)}, f32[2,64,128]{2,1,0:T(8,128)S(1)}, u32[]{:S(2)}, u32[]{:S(2)}) collective-permute-start(f32[2,64,128]{2,1,0:T(8,128)S(1)} %get-tuple-element.58), channel_id=1, source_target_pairs={{0,16},{15,31},{16,0},{31,15},{1,2},{2,1},{3,4},{4,3},{5,6},{6,5},... | collective-permute-start | bytes 196616 | tf_op jit(solution)/shard_map/ppermute | solution.py:756
  30.1 0.9 %shard_map.45 = f32[2,16,4096]{2,1,0:T(8,128)} custom-call(f32[2,704,128]{2,1,0:T(8,128)S(1)} %get-tuple-element.49.b_ref.b0_ref), custom_call_target="tpu_custom_call" | custom-call | flops 4000000 | bytes 500000 | tf_op jit(solution)/shard_map/pallas_call | solution.py:823
  31.0 1.9 %shard_map.47.v3_ref = f32[2,48,128]{2,1,0:T(8,128)S(1)} custom-call(f32[8,2,8,128]{3,2,1,0:T(8,128)S(1)} %all_to_all.5.same_ref, f32[8,2,8,128]{3,2,1,0:T(8,128)S(1)} %collective-permute-done.6.other_ref), custom_call_target="tpu_custom_call" | custom-call | flops 5000000 | bytes 625000 | tf_op jit(solution)/shard_map/pallas_call | solution.py:831
  32.8 0.0 collective-permute-done.8.far_ref
  32.9 2.4 %shard_map.48 = (f32[2,16,4096]{2,1,0:T(8,128)}, f32[2,704,128]{2,1,0:T(8,128)S(1)}) custom-call(f32[2,48,128]{2,1,0:T(8,128)S(1)} %shard_map.47.v3_ref, f32[2,64,128]{2,1,0:T(8,128)S(1)} %collective-permute-done.7.near_ref, f32[2,64,128]{2,1,0:T(8,128)S(1)} %collective-permute-done.8.far_ref, ...), custom_call_target="tpu_custom_call", output_to_operand_aliasing={{1}: (8, {})} | custom-call | tf_op jit(solution)/shard_map/pallas_call | solution.py:838
  (3 shorter events, 0.0 us)
Async XLA Ops:
  2.0 6.3 %collective-permute-start = (f32[4,96,128]{2,1,0:T(8,128)S(1)}, f32[4,96,128]{2,1,0:T(8,128)S(1)}, u32[]{:S(2)}, u32[]{:S(2)}) collective-permute-start(f32[4,96,128]{2,1,0:T(8,128)S(1)} %get-tuple-element.40), channel_id=1, source_target_pairs={{0,1},{1,0},{2,3},{3,2},{4,5},{5,4},{6,7},{7,6},{8,9},{9,8},{10,11... | collective-permute-start | bytes 589832 | tf_op jit(solution)/shard_map/ppermute | solution.py:757
  2.5 6.5 %collective-permute-start.1 = (f32[4,96,128]{2,1,0:T(8,128)S(1)}, f32[4,96,128]{2,1,0:T(8,128)S(1)}, u32[]{:S(2)}, u32[]{:S(2)}) collective-permute-start(f32[4,96,128]{2,1,0:T(8,128)S(1)} %get-tuple-element.48), channel_id=1, source_target_pairs={{0,16},{15,31},{16,0},{31,15},{1,2},{2,1},{3,4},{4,3},{5,6},{6,5},... | collective-permute-start | bytes 589832 | tf_op jit(solution)/shard_map/ppermute | solution.py:756
  6.6 6.7 %collective-permute-start.2 = (f32[2,64,128]{2,1,0:T(8,128)S(1)}, f32[2,64,128]{2,1,0:T(8,128)S(1)}, u32[]{:S(2)}, u32[]{:S(2)}) collective-permute-start(f32[2,64,128]{2,1,0:T(8,128)S(1)} %get-tuple-element.51), channel_id=1, source_target_pairs={{0,1},{1,0},{2,3},{3,2},{4,5},{5,4},{6,7},{7,6},{8,9},{9,8},{10,11... | collective-permute-start | bytes 196616 | tf_op jit(solution)/shard_map/ppermute | solution.py:757
  6.8 6.5 %collective-permute-start.3 = (f32[2,64,128]{2,1,0:T(8,128)S(1)}, f32[2,64,128]{2,1,0:T(8,128)S(1)}, u32[]{:S(2)}, u32[]{:S(2)}) collective-permute-start(f32[2,64,128]{2,1,0:T(8,128)S(1)} %get-tuple-element.52), channel_id=1, source_target_pairs={{0,16},{15,31},{16,0},{31,15},{1,2},{2,1},{3,4},{4,3},{5,6},{6,5},... | collective-permute-start | bytes 196616 | tf_op jit(solution)/shard_map/ppermute | solution.py:756
  9.9 4.0 %collective-permute-start.5 = (f32[2,32,128]{2,1,0:T(8,128)S(1)}, f32[2,32,128]{2,1,0:T(8,128)S(1)}, u32[]{:S(2)}, u32[]{:S(2)}) collective-permute-start(f32[2,32,128]{2,1,0:T(8,128)S(1)} %get-tuple-element.54), channel_id=1, source_target_pairs={{0,16},{15,31},{16,0},{31,15},{1,2},{2,1},{3,4},{4,3},{5,6},{6,5},... | collective-permute-start | bytes 98312 | tf_op jit(solution)/shard_map/ppermute | solution.py:756
  11.6 2.5 %collective-permute-start.4 = (f32[2,32,128]{2,1,0:T(8,128)S(1)}, f32[2,32,128]{2,1,0:T(8,128)S(1)}, u32[]{:S(2)}, u32[]{:S(2)}) collective-permute-start(f32[2,32,128]{2,1,0:T(8,128)S(1)} %get-tuple-element.53), channel_id=1, source_target_pairs={{0,1},{1,0},{2,3},{3,2},{4,5},{5,4},{6,7},{7,6},{8,9},{9,8},{10,11... | collective-permute-start | bytes 98312 | tf_op jit(solution)/shard_map/ppermute | solution.py:757
  28.1 2.9 %collective-permute-start.6 = (f32[8,2,8,128]{3,2,1,0:T(8,128)S(1)}, f32[8,2,8,128]{3,2,1,0:T(8,128)S(1)}, u32[]{:S(2)}, u32[]{:S(2)}) collective-permute-start(f32[8,2,8,128]{3,2,1,0:T(8,128)S(1)} %all_to_all.5.same_ref), channel_id=1, source_target_pairs={{0,1},{1,0},{2,3},{3,2},{4,5},{5,4},{6,7},{7,6},{8,9},{9,8},{10,11... | collective-permute-start | bytes 196616 | tf_op jit(solution)/shard_map/ppermute | solution.py:821
  28.1 4.7 %collective-permute-start.7 = (f32[2,64,128]{2,1,0:T(8,128)S(1)}, f32[2,64,128]{2,1,0:T(8,128)S(1)}, u32[]{:S(2)}, u32[]{:S(2)}) collective-permute-start(f32[2,64,128]{2,1,0:T(8,128)S(1)} %get-tuple-element.57), channel_id=1, source_target_pairs={{0,1},{1,0},{2,3},{3,2},{4,5},{5,4},{6,7},{7,6},{8,9},{9,8},{10,11... | collective-permute-start | bytes 196616 | tf_op jit(solution)/shard_map/ppermute | solution.py:757
  28.6 4.3 %collective-permute-start.8 = (f32[2,64,128]{2,1,0:T(8,128)S(1)}, f32[2,64,128]{2,1,0:T(8,128)S(1)}, u32[]{:S(2)}, u32[]{:S(2)}) collective-permute-start(f32[2,64,128]{2,1,0:T(8,128)S(1)} %get-tuple-element.58), channel_id=1, source_target_pairs={{0,16},{15,31},{16,0},{31,15},{1,2},{2,1},{3,4},{4,3},{5,6},{6,5},... | collective-permute-start | bytes 196616 | tf_op jit(solution)/shard_map/ppermute | solution.py:756
